TPU v7x, 32 devices: a whole 2x2x4 slice. The times are simulated.
32 devices in a mesh: wide: 16 (over z, y, core), narrow: 2 (over x).
Axes of the slice: x: 2, y: 2, z: 4, core: 2. Of those that a mesh axis runs over, the one named last changes fastest.
Arguments:
- tokens: bfloat16 [32, 256, 1120], P(('wide', 'narrow')), may hold values from -6 to 6
- lengths: int32 [32], P(('wide', 'narrow')), may hold values from 128 to 256
- dropped: int32 [32], P(('wide', 'narrow')), may hold values from 0 to 4
- cotangent: bfloat16 [32, 256, 1120], P(('wide', 'narrow')), may hold values from -6 to 6
- first_gain: bfloat16 [1120], P('narrow'), may hold values from 0.5 to 1.5
- first_shift: bfloat16 [1120], P('narrow'), may hold values from -1.5 to 1.5
- qkv_weight: bfloat16 [1120, 3360], P('narrow'), may hold values from -0.1875 to 0.1875
- query_bias: bfloat16 [1120], P('narrow'), may hold values from -2 to 2
- value_bias: bfloat16 [1120], P('narrow'), may hold values from -2 to 2
- out_weight: bfloat16 [1120, 1120], P('narrow'), may hold values from -1.5 to 1.5
- out_bias: bfloat16 [1120], P('narrow'), may hold values from -1.5 to 1.5
- second_gain: bfloat16 [1120], P('narrow'), may hold values from 0.5 to 1.5
- second_shift: bfloat16 [1120], P('narrow'), may hold values from -1.5 to 1.5
- up_weight: bfloat16 [1120, 4480], P('narrow'), may hold values from -0.1875 to 0.1875
- up_bias: bfloat16 [4480], P('narrow'), may hold values from -2 to 2
- down_weight: bfloat16 [4480, 1120], P('narrow'), may hold values from -0.1875 to 0.1875
- down_bias: bfloat16 [1120], P('narrow'), may hold values from -1.5 to 1.5
Outputs:
- output: bfloat16 [32, 256, 1120], P(('wide', 'narrow'))
- grad_tokens: float32 [32, 256, 1120], P(('wide', 'narrow'))
- grad_first_gain: float32 [1120], P('narrow')
- grad_first_shift: float32 [1120], P('narrow')
- grad_qkv_weight: float32 [1120, 3360], P('narrow', 'wide')
- grad_query_bias: float32 [1120], P('narrow')
- grad_value_bias: float32 [1120], P('narrow')
- grad_out_weight: float32 [1120, 1120], P('narrow', 'wide')
- grad_out_bias: float32 [1120], P('narrow')
- grad_second_gain: float32 [1120], P('narrow')
- grad_second_shift: float32 [1120], P('narrow')
- grad_up_weight: float32 [1120, 4480], P('narrow', 'wide')
- grad_up_bias: float32 [4480], P('narrow')
- grad_down_weight: float32 [4480, 1120], P('narrow', 'wide')
- grad_down_bias: float32 [1120], P('narrow')
All inputs are finite; a program needn't handle non-finite values.
Results may differ from a plain program's by a relative error of at most 0.018.
Values may be sent and summed in bfloat16 or wider, within the bound.
A program may use at most 192 MiB of HBM per device.

v0:
```python
import jax
import jax.numpy as jnp
from jax import lax
from jax.sharding import PartitionSpec as P

HEAD = 56


epsilon = 1e-05
head_groups = 4


def normed(values, gain, shift):
    center = values - jnp.mean(values, axis=-1, keepdims=True)
    spread = jnp.mean(center * center, axis=-1, keepdims=True)
    return center * lax.rsqrt(spread + epsilon) * gain + shift


def split_heads(matrix):
    rows = matrix.shape[0]
    return matrix.reshape(rows, head_groups, -1, HEAD).transpose(1, 0, 2, 3)


def join_heads(blocks):
    return blocks.transpose(1, 0, 2, 3).reshape(blocks.shape[1], -1)


def key_mask(length, drop, rows):
    places = jnp.arange(rows, dtype=jnp.int32)
    live = (places < length) & ((places < 1) | (places > drop))
    return (places[None, :] <= places[:, None]) & (
        live[None, :] | (places[None, :] == places[:, None])
    )


def scores_of(query, keys, mask):
    raw = jnp.einsum("qhe,khe->hqk", query, keys, preferred_element_type=jnp.float32) * HEAD ** (
        -0.5
    )
    return jnp.where(mask[None], raw, -jnp.inf)


def forward(inputs, weights, mask):
    (
        first_gain,
        first_shift,
        qkv_weight,
        query_bias,
        value_bias,
        out_weight,
        out_bias,
        second_gain,
        second_shift,
        up_weight,
        up_bias,
        down_weight,
        down_bias,
    ) = weights
    width = inputs.shape[1]
    first = normed(inputs, first_gain.astype(jnp.float32), first_shift.astype(jnp.float32)).astype(
        jnp.bfloat16
    )
    mixed = jnp.dot(first, qkv_weight, preferred_element_type=jnp.float32)
    query = (mixed[:, :width] + query_bias).astype(jnp.bfloat16)
    keys = mixed[:, width : 2 * width].astype(jnp.bfloat16)
    values = (mixed[:, 2 * width :] + value_bias).astype(jnp.bfloat16)

    def attend(group):
        scores = scores_of(group[0], group[1], mask)
        top = jnp.max(scores, axis=-1, keepdims=True)
        expos = jnp.exp(scores - top)
        total = jnp.sum(expos, axis=-1, keepdims=True)
        probs = (expos / total).astype(jnp.bfloat16)
        heads_out = jnp.einsum("hqk,khe->qhe", probs, group[2], preferred_element_type=jnp.float32)
        return (heads_out.astype(jnp.bfloat16), top + jnp.log(total))

    heads_out, logsum = lax.map(
        attend, (split_heads(query), split_heads(keys), split_heads(values))
    )
    attended = join_heads(heads_out)
    middle = inputs + (jnp.dot(attended, out_weight, preferred_element_type=jnp.float32) + out_bias)
    second = normed(
        middle, second_gain.astype(jnp.float32), second_shift.astype(jnp.float32)
    ).astype(jnp.bfloat16)
    hidden = jnp.dot(second, up_weight, preferred_element_type=jnp.float32) + up_bias
    active = jax.nn.gelu(hidden, approximate=True).astype(jnp.bfloat16)
    result = middle + (jnp.dot(active, down_weight, preferred_element_type=jnp.float32) + down_bias)
    kept = (first, query, keys, values, logsum, attended, middle, second, hidden, active)
    return (result, kept)


def local(
    tokens,
    lengths,
    dropped,
    cotangent,
    first_gain,
    first_shift,
    qkv_weight,
    query_bias,
    value_bias,
    out_weight,
    out_bias,
    second_gain,
    second_shift,
    up_weight,
    up_bias,
    down_weight,
    down_bias,
):
    rows = tokens.shape[1]
    mask = key_mask(lengths[0], dropped[0], rows)
    inputs = tokens[0].astype(jnp.float32)
    full = (
        lax.all_gather(first_gain, "narrow", axis=0, tiled=True),
        lax.all_gather(first_shift, "narrow", axis=0, tiled=True),
        lax.all_gather(qkv_weight, "narrow", axis=0, tiled=True),
        lax.all_gather(query_bias, "narrow", axis=0, tiled=True),
        lax.all_gather(value_bias, "narrow", axis=0, tiled=True),
        lax.all_gather(out_weight, "narrow", axis=0, tiled=True),
        lax.all_gather(out_bias, "narrow", axis=0, tiled=True),
        lax.all_gather(second_gain, "narrow", axis=0, tiled=True),
        lax.all_gather(second_shift, "narrow", axis=0, tiled=True),
        lax.all_gather(up_weight, "narrow", axis=0, tiled=True),
        lax.all_gather(up_bias, "narrow", axis=0, tiled=True),
        lax.all_gather(down_weight, "narrow", axis=0, tiled=True),
        lax.all_gather(down_bias, "narrow", axis=0, tiled=True),
    )
    result, unused = forward(inputs, full, mask)
    output = result.astype(jnp.bfloat16)[None]
    again = (
        lax.all_gather(first_gain, "narrow", axis=0, tiled=True),
        lax.all_gather(first_shift, "narrow", axis=0, tiled=True),
        lax.all_gather(qkv_weight, "narrow", axis=0, tiled=True),
        lax.all_gather(query_bias, "narrow", axis=0, tiled=True),
        lax.all_gather(value_bias, "narrow", axis=0, tiled=True),
        lax.all_gather(out_weight, "narrow", axis=0, tiled=True),
        lax.all_gather(out_bias, "narrow", axis=0, tiled=True),
        lax.all_gather(second_gain, "narrow", axis=0, tiled=True),
        lax.all_gather(second_shift, "narrow", axis=0, tiled=True),
        lax.all_gather(up_weight, "narrow", axis=0, tiled=True),
        lax.all_gather(up_bias, "narrow", axis=0, tiled=True),
        lax.all_gather(down_weight, "narrow", axis=0, tiled=True),
        lax.all_gather(down_bias, "narrow", axis=0, tiled=True),
    )
    (
        w_gain1,
        w_shift1,
        w_qkv,
        w_query,
        w_value,
        w_out,
        w_outb,
        w_gain2,
        w_shift2,
        w_up,
        w_upb,
        w_down,
        w_downb,
    ) = again
    result, kept = forward(inputs, again, mask)
    first, query, keys, values, logsum, attended, middle, second, hidden, active = kept
    grad_out = cotangent[0]
    d_down = jnp.dot(active.T, grad_out, preferred_element_type=jnp.float32)
    d_downb = jnp.sum(grad_out.astype(jnp.float32), axis=0)
    d_active = jnp.dot(grad_out, w_down.T, preferred_element_type=jnp.float32)
    unused, gelu_pull = jax.vjp(lambda v: jax.nn.gelu(v, approximate=True), hidden)
    d_hidden = gelu_pull(d_active)[0].astype(jnp.bfloat16)
    d_up = jnp.dot(second.T, d_hidden, preferred_element_type=jnp.float32)
    d_upb = jnp.sum(d_hidden.astype(jnp.float32), axis=0)
    d_second = jnp.dot(d_hidden, w_up.T, preferred_element_type=jnp.float32)
    unused, norm_pull = jax.vjp(
        normed, middle, w_gain2.astype(jnp.float32), w_shift2.astype(jnp.float32)
    )
    d_middle, d_gain2, d_shift2 = norm_pull(d_second)
    d_middle = d_middle + grad_out.astype(jnp.float32)
    d_branch = d_middle.astype(jnp.bfloat16)
    d_outw = jnp.dot(attended.T, d_branch, preferred_element_type=jnp.float32)
    d_outb = jnp.sum(d_branch.astype(jnp.float32), axis=0)
    d_attended = jnp.dot(d_branch, w_out.T, preferred_element_type=jnp.float32).astype(jnp.bfloat16)

    def attend_back(group):
        q_part, k_part, v_part, lse_part, do_part = group
        scores = scores_of(q_part, k_part, mask)
        probs = jnp.exp(scores - lse_part)
        rounded = probs.astype(jnp.bfloat16)
        d_v = jnp.einsum("hqk,qhe->khe", rounded, do_part, preferred_element_type=jnp.float32)
        d_probs = jnp.einsum("qhe,khe->hqk", do_part, v_part, preferred_element_type=jnp.float32)
        inner = jnp.sum(d_probs * probs, axis=-1, keepdims=True)
        d_scores = (probs * (d_probs - inner)).astype(jnp.bfloat16)
        d_q = jnp.einsum(
            "hqk,khe->qhe", d_scores, k_part, preferred_element_type=jnp.float32
        ) * HEAD ** (-0.5)
        d_k = jnp.einsum(
            "hqk,qhe->khe", d_scores, q_part, preferred_element_type=jnp.float32
        ) * HEAD ** (-0.5)
        return (d_q.astype(jnp.bfloat16), d_k.astype(jnp.bfloat16), d_v.astype(jnp.bfloat16))

    d_qs, d_ks, d_vs = lax.map(
        attend_back,
        (
            split_heads(query),
            split_heads(keys),
            split_heads(values),
            logsum,
            split_heads(d_attended),
        ),
    )
    d_query = join_heads(d_qs)
    d_values = join_heads(d_vs)
    d_mixed = jnp.concatenate([d_query, join_heads(d_ks), d_values], axis=1)
    d_queryb = jnp.sum(d_query.astype(jnp.float32), axis=0)
    d_valueb = jnp.sum(d_values.astype(jnp.float32), axis=0)
    d_qkv = jnp.dot(first.T, d_mixed, preferred_element_type=jnp.float32)
    d_first = jnp.dot(d_mixed, w_qkv.T, preferred_element_type=jnp.float32)
    unused, first_pull = jax.vjp(
        normed, inputs, w_gain1.astype(jnp.float32), w_shift1.astype(jnp.float32)
    )
    d_inputs, d_gain1, d_shift1 = first_pull(d_first)
    grad_tokens = (d_middle + d_inputs)[None]
    parted = (
        lax.psum_scatter(
            d_gain1.astype(jnp.bfloat16), "narrow", scatter_dimension=0, tiled=True
        ).astype(jnp.float32),
        lax.psum_scatter(
            d_shift1.astype(jnp.bfloat16), "narrow", scatter_dimension=0, tiled=True
        ).astype(jnp.float32),
        lax.psum_scatter(
            d_qkv.astype(jnp.bfloat16), "narrow", scatter_dimension=0, tiled=True
        ).astype(jnp.float32),
        lax.psum_scatter(
            d_queryb.astype(jnp.bfloat16), "narrow", scatter_dimension=0, tiled=True
        ).astype(jnp.float32),
        lax.psum_scatter(
            d_valueb.astype(jnp.bfloat16), "narrow", scatter_dimension=0, tiled=True
        ).astype(jnp.float32),
        lax.psum_scatter(
            d_outw.astype(jnp.bfloat16), "narrow", scatter_dimension=0, tiled=True
        ).astype(jnp.float32),
        lax.psum_scatter(
            d_outb.astype(jnp.bfloat16), "narrow", scatter_dimension=0, tiled=True
        ).astype(jnp.float32),
        lax.psum_scatter(
            d_gain2.astype(jnp.bfloat16), "narrow", scatter_dimension=0, tiled=True
        ).astype(jnp.float32),
        lax.psum_scatter(
            d_shift2.astype(jnp.bfloat16), "narrow", scatter_dimension=0, tiled=True
        ).astype(jnp.float32),
        lax.psum_scatter(
            d_up.astype(jnp.bfloat16), "narrow", scatter_dimension=0, tiled=True
        ).astype(jnp.float32),
        lax.psum_scatter(
            d_upb.astype(jnp.bfloat16), "narrow", scatter_dimension=0, tiled=True
        ).astype(jnp.float32),
        lax.psum_scatter(
            d_down.astype(jnp.bfloat16), "narrow", scatter_dimension=0, tiled=True
        ).astype(jnp.float32),
        lax.psum_scatter(
            d_downb.astype(jnp.bfloat16), "narrow", scatter_dimension=0, tiled=True
        ).astype(jnp.float32),
    )
    mats = (
        lax.psum_scatter(
            parted[2].astype(jnp.bfloat16), "wide", scatter_dimension=1, tiled=True
        ).astype(jnp.float32),
        lax.psum_scatter(
            parted[5].astype(jnp.bfloat16), "wide", scatter_dimension=1, tiled=True
        ).astype(jnp.float32),
        lax.psum_scatter(
            parted[9].astype(jnp.bfloat16), "wide", scatter_dimension=1, tiled=True
        ).astype(jnp.float32),
        lax.psum_scatter(
            parted[11].astype(jnp.bfloat16), "wide", scatter_dimension=1, tiled=True
        ).astype(jnp.float32),
    )
    vecs = lax.psum(
        (
            parted[0],
            parted[1],
            parted[3],
            parted[4],
            parted[6],
            parted[7],
            parted[8],
            parted[10],
            parted[12],
        ),
        "wide",
    )
    summed = (
        vecs[0],
        vecs[1],
        mats[0],
        vecs[2],
        vecs[3],
        mats[1],
        vecs[4],
        vecs[5],
        vecs[6],
        mats[2],
        vecs[7],
        mats[3],
        vecs[8],
    )
    return (
        output,
        grad_tokens,
        summed[0],
        summed[1],
        summed[2],
        summed[3],
        summed[4],
        summed[5],
        summed[6],
        summed[7],
        summed[8],
        summed[9],
        summed[10],
        summed[11],
        summed[12],
    )


def solution(mesh):
    return jax.shard_map(
        local,
        mesh=mesh,
        in_specs=(
            P(("wide", "narrow"), None, None),
            P(("wide", "narrow")),
            P(("wide", "narrow")),
            P(("wide", "narrow"), None, None),
            P("narrow"),
            P("narrow"),
            P("narrow", None),
            P("narrow"),
            P("narrow"),
            P("narrow", None),
            P("narrow"),
            P("narrow"),
            P("narrow"),
            P("narrow", None),
            P("narrow"),
            P("narrow", None),
            P("narrow"),
        ),
        out_specs=(
            P(("wide", "narrow"), None, None),
            P(("wide", "narrow"), None, None),
            P("narrow"),
            P("narrow"),
            P("narrow", "wide"),
            P("narrow"),
            P("narrow"),
            P("narrow", "wide"),
            P("narrow"),
            P("narrow"),
            P("narrow"),
            P("narrow", "wide"),
            P("narrow"),
            P("narrow", "wide"),
            P("narrow"),
        ),
        check_vma=False,
    )
```

profile of v0, /device:TPU:0, one launch (start us, length us, event | category | flops | bytes accessed | tf_op | source)
XLA Modules:
  0.0 1110.8 jit_solution(9978614819374630584)
XLA Ops:
  14.1 10.1 all-reduce.26
  26.1 82.9 %all-gather.5.cloned.1.call-done = bf16[1120,3360]{1,0:T(8,128)(2,1)} async-done(((bf16[560,3360]{1,0:T(8,128)(2,1)}), bf16[1120,3360]{1,0:T(8,128)(2,1)}) %all-gather.5.cloned.1.call-update) | async-done | bytes 7526416 | tf_op jit(solution)/shard_map/all_gather | solution.py:117
  109.0 6.8 fusion.162
  116.3 4.6 while.40
  120.9 28.1 %all-gather.7.cloned.1.call-done = bf16[1120,1120]{1,0:T(8,128)(2,1)} async-done(((bf16[560,1120]{1,0:T(8,128)(2,1)}), bf16[1120,1120]{1,0:T(8,128)(2,1)}) %all-gather.7.cloned.1.call-update) | async-done | bytes 2508816 | tf_op jit(solution)/shard_map/all_gather | solution.py:120
  149.1 3.2 fusion.175
  152.5 122.7 %all-gather.9.cloned.1.call-done = bf16[1120,4480]{1,0:T(8,128)(2,1)} async-done(((bf16[560,4480]{1,0:T(8,128)(2,1)}), bf16[1120,4480]{1,0:T(8,128)(2,1)}) %all-gather.9.cloned.1.call-update) | async-done | bytes 10035216 | tf_op jit(solution)/shard_map/all_gather | solution.py:124
  275.2 9.7 convolution_add_fusion
  284.9 119.4 %all-gather.11.cloned.1.call-done = bf16[4480,1120]{1,0:T(8,128)(2,1)} async-done(((bf16[2240,1120]{1,0:T(8,128)(2,1)}), bf16[4480,1120]{1,0:T(8,128)(2,1)}) %all-gather.11.cloned.1.call-update) | async-done | bytes 10035216 | tf_op jit(solution)/shard_map/all_gather | solution.py:126
  404.4 12.2 %fusion.176 = (bf16[4480]{0:T(1024)(128)(2,1)}, bf16[256,4480]{1,0:T(8,128)(2,1)S(1)}) fusion(f32[256,4480]{1,0:T(8,128)} %convolution_add_fusion, bf16[4480,1120]{1,0:T(8,128)(2,1)} %all-gather.11.cloned.1.call-done, bf16[1,256,1120]{1,2,0:T(8,128)(2,1)S(1)} %copy-done.4), kind=kOutput, calls=%fused_computation.218 | convolution fusion | flops 2593091072 | bytes 17498880 | tf_op jit(solution)/shard_map/dot_general | solution.py:166
  416.6 3.8 multiply_reduce_fusion.1
  423.2 2.4 convolution_convert_fusion.6
  425.9 3.6 convolution_convert_fusion.7
  432.0 28.2 %while.41 = (s32[]{:T(128)}, bf16[4,256,5,56]{1,3,2,0:T(8,128)(2,1)}, bf16[4,256,5,56]{1,3,2,0:T(8,128)(2,1)}, bf16[4,256,5,56]{1,3,2,0:T(8,128)(2,1)}, bf16[4,2...) while((s32[]{:T(128)}, ...), condition=%wide.region_18.19_spmd.clone, body=%wide.region_16.18_spmd.clone.sunk | while | flops 187069184 | bytes 13723029 | solution.py:199
  432.1 1.6 fusion.245
  433.8 1.3 multiply_reduce_fusion.6
  436.2 1.9 fusion.247
  439.3 1.5 fusion.245
  440.8 1.3 multiply_reduce_fusion.6
  443.3 1.9 fusion.247
  446.3 1.5 fusion.245
  447.8 1.3 multiply_reduce_fusion.6
  450.3 1.9 fusion.247
  453.3 1.5 fusion.245
  454.8 1.3 multiply_reduce_fusion.6
  457.3 1.9 fusion.247
  460.2 6.1 convolution_convert_fusion.5
  466.4 7.7 convolution_convert_fusion.4
  475.2 10.2 convolution_convert_fusion.3
  490.8 69.0 %reduce-scatter.11.cloned.1.call-done = bf16[560,3360]{1,0:T(8,128)(2,1)} async-done(((bf16[1120,3360]{1,0:T(8,128)(2,1)}), bf16[560,3360]{1,0:T(8,128)(2,1)}) %reduce-scatter.11.cloned.1.call-update) | async-done | bytes 3763216 | tf_op jit(solution)/shard_map/reduce_scatter | solution.py:228
  559.8 130.1 %reduce-scatter.17.cloned.1.call-done = bf16[560,4480]{1,0:T(8,128)(2,1)} async-done(((bf16[1120,4480]{1,0:T(8,128)(2,1)}), bf16[560,4480]{1,0:T(8,128)(2,1)}) %reduce-scatter.17.cloned.1.call-update) | async-done | bytes 5017616
  689.9 123.0 %reduce-scatter.15.cloned.1.call-done = bf16[2240,1120]{1,0:T(8,128)(2,1)} async-done(((bf16[4480,1120]{1,0:T(8,128)(2,1)}), bf16[2240,1120]{1,0:T(8,128)(2,1)}) %reduce-scatter.15.cloned.1.call-update) | async-done | bytes 5017616 | tf_op jit(solution)/shard_map/reduce_scatter | solution.py:255
  814.2 14.7 %while.39 = (s32[]{:T(128)}, bf16[4,256,5,56]{1,3,2,0:T(8,128)(2,1)}, bf16[4,256,5,56]{1,3,2,0:T(8,128)(2,1)}, bf16[4,256,5,56]{1,3,2,0:T(8,128)(2,1)S(1)}, bf16...) while((s32[]{:T(128)}, bf16[4,256,5,56]{1,3,2,0:T(8,128)(2,1)}, ...), condition=%wide.region_5.6_spmd.clone, body=%wide.region_2.5_spmd.clone.sunk | while | flops 113385216 | bytes 1073493 | solution.py:77
  815.5 2.3 fusion.230
  819.2 2.3 fusion.230
  821.6 1.2 fusion.229
  822.8 2.4 fusion.230
  826.5 2.3 fusion.230
  828.9 3.1 fusion.177
  834.4 5.7 fusion.164
  841.8 7.6 all-reduce.25
  850.1 64.2 %all-reduce.23 = (f32[560]{0:T(1024)}, f32[560]{0:T(1024)}, f32[560]{0:T(1024)}, f32[560]{0:T(1024)}, f32[560]{0:T(1024)}, /*index=5*/f32[560]{0:T(1024)}, f32[560]{0:T(1024)}, f32[2240]{0:T(1024)}, f32[560]{0:T(1024)}) all-reduce(f32[560]{0:T(1024)S(1)} %dynamic-slice_convert_fusion.12, ...), channel_id=1, replica_groups=mesh['wide'=16,'narrow'=2] {'wide'}, use_global_device_ids=true, to_apply=%region_23.24 | all-reduce | flops 6720 | bytes 53760 | tf_op jit(solution)/shard_map/psum | solution.py:276
  914.3 2.7 add_bitcast_fusion
  917.1 15.4 %fusion.114 = bf16[1,256,1120]{1,2,0:T(8,128)(2,1)} fusion(f32[256,1120]{0,1:T(8,128)} %copy-done.16, bf16[4480,1120]{1,0:T(8,128)(2,1)} %all-gather.11.cloned.1.call-done, bf16[1120,4480]{1,0:T(8,128)(2,1)} %all-gather.9.cloned.1.call-done, f32[4480]{0:T(1024)S(1)} %convert_element_type.220, f32[1120]{0:T(1024)S(1)} %convert_element_type.222, ...), kind=kOutput, calls=%fused_computation.127 | convolution fusion | flops 5151784960 | bytes 21824128 | tf_op jit(solution)/shard_map/dot_general | solution.py:87
  932.5 162.4 %all-reduce.29.cloned.1.call-done = (bf16[560,3360]{1,0:T(8,128)(2,1)}, bf16[560,1120]{1,0:T(8,128)(2,1)}, bf16[560,4480]{1,0:T(8,128)(2,1)}, bf16[2240,1120]{1,0:T(8,128)(2,1)}) async-done(((bf16[560,3360]{1,0:T(8,128)(2,1)}, bf16[560,1120]{1,0:T(8,128)(2,1)}, bf16[560,4480]{1,0:T(8,128)(2,1)}, bf16[2240,1120]{1,0:T(8,128)(2,1)}), (bf16[560,3360]{1,0:T(8,128)(2,1)}, bf16[560,1120]{1,0:T(8,128)(2,1)}, ...) | async-done | bytes 15052816
  1099.0 1.3 dynamic-slice_convert_fusion.1
  1101.4 1.5 dynamic-slice_convert_fusion
  1102.9 1.2 copy.58
  (241 shorter events, 43.9 us)
Async XLA Ops:
  7.2 101.8 %all-gather.5.cloned.1.call-start = ((), (), s32[]{:S(2)}) async-start(), calls=%async_computation.4 | async-start | bytes 11612160 | tf_op jit(solution)/shard_map/all_gather | solution.py:117
  7.9 141.2 %all-gather.7.cloned.1.call-start = ((), (), s32[]{:S(2)}) async-start(), calls=%async_computation.5 | async-start | bytes 3870720 | tf_op jit(solution)/shard_map/all_gather | solution.py:120
  8.7 266.6 %all-gather.9.cloned.1.call-start = ((), (), s32[]{:S(2)}) async-start(), calls=%async_computation.6 | async-start | bytes 15052800 | tf_op jit(solution)/shard_map/all_gather | solution.py:124
  9.4 2.7 copy-start.38
  9.4 2.9 copy-start.39
  9.4 3.1 copy-start.40
  9.4 3.4 copy-start.41
  9.5 3.6 copy-start.42
  9.5 3.8 copy-start.43
  9.5 4.1 copy-start.44
  9.5 4.3 copy-start.34
  9.5 16.1 %copy-start.1 = (bf16[1,256,1120]{1,2,0:T(8,128)(2,1)S(1)}, bf16[1,256,1120]{1,2,0:T(8,128)(2,1)}, u32[]{:S(2)}) copy-start(bf16[1,256,1120]{1,2,0:T(8,128)(2,1)} %param.23) | copy-start | bytes 1720324
  9.5 394.9 %all-gather.11.cloned.1.call-start = ((), (), s32[]{:S(2)}) async-start(), calls=%async_computation.7 | async-start | bytes 15482880 | tf_op jit(solution)/shard_map/all_gather | solution.py:126
  10.1 480.7 %reduce-scatter.13.cloned.1.call-start = ((), (), s32[]{:S(2)}) async-start(), calls=%async_computation.9 | async-start | bytes 3870720 | tf_op jit(solution)/shard_map/reduce_scatter | solution.py:237
  24.2 124.9 %copy-start.31 = (f32[1120]{0:T(1024)}, f32[1120]{0:T(1024)S(1)}, u32[]{:S(2)}) copy-start(f32[1120]{0:T(1024)S(1)} %convert_element_type.216) | copy-start | bytes 13444
  24.2 91.6 %copy-start.32 = (f32[1120]{0:T(1024)}, f32[1120]{0:T(1024)S(1)}, u32[]{:S(2)}) copy-start(f32[1120]{0:T(1024)S(1)} %convert_element_type.210) | copy-start | bytes 13444
  25.8 434.4 %copy-start.21 = (f32[256]{0:T(256)}, f32[256]{0:T(256)S(1)}, u32[]{:S(2)}) copy-start(f32[256]{0:T(256)S(1)} %broadcast_multiply_fusion.2) | copy-start | bytes 3076
  26.1 89.8 %copy-start.26 = (f32[256]{0:T(256)}, f32[256]{0:T(256)S(1)}, u32[]{:S(2)}) copy-start(f32[256]{0:T(256)S(1)} %fusion.129) | copy-start | bytes 3076
  26.1 89.8 %copy-start.28 = (f32[256]{0:T(256)}, f32[256]{0:T(256)S(1)}, u32[]{:S(2)}) copy-start(f32[256]{0:T(256)S(1)} %fusion.149) | copy-start | bytes 3076
  120.9 28.2 %copy-start.9 = (bf16[4,256,5,56]{1,3,2,0:T(8,128)(2,1)}, bf16[4,256,5,56]{1,3,2,0:T(8,128)(2,1)S(1)}, u32[]{:S(2)}) copy-start(bf16[4,256,5,56]{1,3,2,0:T(8,128)(2,1)S(1)} %get-tuple-element.620) | copy-start | bytes 1720324
  120.9 28.2 %copy-start.11 = (bf16[4,256,5,56]{1,3,2,0:T(8,128)(2,1)}, bf16[4,256,5,56]{1,3,2,0:T(8,128)(2,1)S(1)}, u32[]{:S(2)}) copy-start(bf16[4,256,5,56]{1,3,2,0:T(8,128)(2,1)S(1)} %get-tuple-element.140) | copy-start | bytes 1720324
  120.9 164.0 %copy-start.2 = (bf16[4,256,5,56]{1,3,2,0:T(8,128)(2,1)}, bf16[4,256,5,56]{1,3,2,0:T(8,128)(2,1)S(1)}, u32[]{:S(2)}) copy-start(bf16[4,256,5,56]{1,3,2,0:T(8,128)(2,1)S(1)} %get-tuple-element.605) | copy-start | bytes 1720324
  152.5 251.9 %copy-start.4 = (bf16[1,256,1120]{1,2,0:T(8,128)(2,1)S(1)}, bf16[1,256,1120]{1,2,0:T(8,128)(2,1)}, u32[]{:S(2)}) copy-start(bf16[1,256,1120]{1,2,0:T(8,128)(2,1)} %param.26) | copy-start | bytes 1720324
  404.4 12.2 %copy-start = (bf16[1120,4480]{1,0:T(8,128)(2,1)S(1)}, bf16[1120,4480]{1,0:T(8,128)(2,1)}, u32[]{:S(2)}) copy-start(bf16[1120,4480]{1,0:T(8,128)(2,1)} %all-gather.9.cloned.1.call-done) | copy-start | bytes 30105604
  416.6 3.8 copy-start.15
  420.8 2.4 copy-start.12
  420.8 4.8 copy-start.24
  425.6 134.2 %reduce-scatter.11.cloned.1.call-start = ((), (), s32[]{:S(2)}) async-start(), calls=%async_computation.8 | async-start | bytes 11612160 | tf_op jit(solution)/shard_map/reduce_scatter | solution.py:228
  432.0 28.2 %copy-start.29 = (f32[256]{0:T(256)S(1)}, f32[256]{0:T(256)}, u32[]{:S(2)}) copy-start(f32[256]{0:T(256)} %copy-done.28) | copy-start | bytes 3076
  432.0 28.2 %copy-start.33 = (f32[1120]{0:T(1024)S(1)}, f32[1120]{0:T(1024)}, u32[]{:S(2)}) copy-start(f32[1120]{0:T(1024)} %copy-done.32) | copy-start | bytes 13444
  432.0 1.8 copy-start.8
  466.3 223.6 %reduce-scatter.17.cloned.1.call-start = ((), (), s32[]{:S(2)}) async-start(), calls=%async_computation.11 | async-start | bytes 15052800
  474.1 338.8 %reduce-scatter.15.cloned.1.call-start = ((), (), s32[]{:S(2)}) async-start(), calls=%async_computation.10 | async-start | bytes 15482880 | tf_op jit(solution)/shard_map/reduce_scatter | solution.py:255
  485.3 2.6 copy-start.47
  485.3 5.2 copy-start.45
  485.4 609.5 %all-reduce.29.cloned.1.call-start = ((), (), s32[]{:S(2)}) async-start(), calls=%async_computation.12 | async-start | bytes 30679040
  490.8 322.1 %copy-start.19 = (bf16[1120]{0:T(1024)(128)(2,1)}, bf16[1120]{0:T(1024)(128)(2,1)S(1)}, u32[]{:S(2)}) copy-start(bf16[1120]{0:T(1024)(128)(2,1)S(1)} %dynamic-update-slice.8) | copy-start | bytes 6724
  832.0 1.8 copy-start.13
  832.0 1.8 copy-start.14
  832.0 2.3 copy-start.22
  834.4 5.8 copy-start.27
  834.4 6.7 copy-start.30
  840.1 1.6 copy-start.17
  840.1 1.6 copy-start.18
  840.1 1.6 copy-start.20
  840.2 1.6 copy-start.23
  840.2 74.1 %copy-start.25 = (f32[256]{0:T(256)S(1)}, f32[256]{0:T(256)}, u32[]{:S(2)}) copy-start(f32[256]{0:T(256)} %copy-done.24) | copy-start | bytes 3076
  914.3 2.7 copy-start.46
  (12 other events, 15.0 us)
Sparse Core Ops, SparseCore 0:
  9.5 99.4 all-gather.4
  110.5 38.5 all-gather.6
  150.7 124.5 all-gather.8
  276.6 127.6 all-gather.10
  425.7 37.2 reduce-scatter.12
  466.5 93.2 reduce-scatter.10
  562.1 127.7 reduce-scatter.16
  692.2 120.6 reduce-scatter.14
  817.5 277.2 all-reduce.28
where the time goes:
time: 1120 us; the launch traced here: 1110 us
  waiting for transfers between devices  840 us (75%)
  matrix products  134 us (12%)
  blocking collectives  81.9 us (7%)
  between operations  20.6 us (2%)
  local copies, waits for them, and re-layouts  16.4 us (1%)
  other arithmetic  16.3 us (1%)
    unnamed x11, waiting for transfers between devices  295 us
    reduce_scatter x1, waiting for transfers between devices, local(): lax.psum_scatter(d_down.astype(jnp.bfloat16), 'narrow', scatter_dimension...  123 us
    all_gather x1, waiting for transfers between devices, local(): lax.all_gather(up_weight, 'narrow', axis=0, tiled=True)  123 us
    all_gather x1, waiting for transfers between devices, local(): lax.all_gather(down_weight, 'narrow', axis=0, tiled=True)  119 us
    all_gather x1, waiting for transfers between devices, local(): lax.all_gather(qkv_weight, 'narrow', axis=0, tiled=True)  82.9 us
    reduce_scatter x1, waiting for transfers between devices, local(): lax.psum_scatter(d_qkv.astype(jnp.bfloat16), 'narrow', scatter_dimension=...  69 us
    psum x1, blocking collectives, local(): lax.psum((parted[0], parted[1], parted[3], parted[4], parted[6], parted[7...  64.2 us
    all_gather x1, waiting for transfers between devices, local(): lax.all_gather(out_weight, 'narrow', axis=0, tiled=True)  28.1 us
  transfers between devices with their start and end apart: 9, of which 8 were waited for; matrix products, arithmetic and copies ran while one was open for 12% of the time, Pallas kernels for 0%

commit v1 on v0

v1 whole, which is shorter than its diff:
```python
import jax
import jax.numpy as jnp
from jax import lax
from jax.sharding import PartitionSpec as P

HEAD = 56
epsilon = 1e-05
head_groups = 4
AXES = ("wide", "narrow")
f32 = jnp.float32
bf16 = jnp.bfloat16


def dot(left, right):
    return jnp.dot(left, right, preferred_element_type=f32)


def tdot(left, right):
    return lax.dot_general(left, right, (((0,), (0,)), ((), ())), preferred_element_type=f32)


def dot_t(left, right):
    return lax.dot_general(left, right, (((1,), (1,)), ((), ())), preferred_element_type=f32)


def normed(values, gain, shift):
    center = values - jnp.mean(values, axis=-1, keepdims=True)
    spread = jnp.mean(center * center, axis=-1, keepdims=True)
    return center * lax.rsqrt(spread + epsilon) * gain + shift


def split_heads(matrix):
    rows = matrix.shape[0]
    return matrix.reshape(rows, head_groups, -1, HEAD).transpose(1, 0, 2, 3)


def join_heads(blocks):
    return blocks.transpose(1, 0, 2, 3).reshape(blocks.shape[1], -1)


def key_mask(length, drop, rows):
    places = jnp.arange(rows, dtype=jnp.int32)
    live = (places < length) & ((places < 1) | (places > drop))
    return (places[None, :] <= places[:, None]) & (
        live[None, :] | (places[None, :] == places[:, None])
    )


def scores_of(query, keys, mask):
    raw = jnp.einsum("qhe,khe->hqk", query, keys, preferred_element_type=f32) * HEAD ** (-0.5)
    return jnp.where(mask[None], raw, -jnp.inf)


def attention(query, keys, values, mask):
    def attend(group):
        scores = scores_of(group[0], group[1], mask)
        top = jnp.max(scores, axis=-1, keepdims=True)
        expos = jnp.exp(scores - top)
        total = jnp.sum(expos, axis=-1, keepdims=True)
        probs = (expos / total).astype(bf16)
        heads_out = jnp.einsum("hqk,khe->qhe", probs, group[2], preferred_element_type=f32)
        return (heads_out.astype(bf16), top + jnp.log(total))

    heads_out, logsum = lax.map(
        attend, (split_heads(query), split_heads(keys), split_heads(values))
    )
    return join_heads(heads_out), logsum


def attention_back(query, keys, values, logsum, d_attended, mask):
    def attend_back(group):
        q_part, k_part, v_part, lse_part, do_part = group
        scores = scores_of(q_part, k_part, mask)
        probs = jnp.exp(scores - lse_part)
        rounded = probs.astype(bf16)
        d_v = jnp.einsum("hqk,qhe->khe", rounded, do_part, preferred_element_type=f32)
        d_probs = jnp.einsum("qhe,khe->hqk", do_part, v_part, preferred_element_type=f32)
        inner = jnp.sum(d_probs * probs, axis=-1, keepdims=True)
        d_scores = (probs * (d_probs - inner)).astype(bf16)
        d_q = jnp.einsum("hqk,khe->qhe", d_scores, k_part, preferred_element_type=f32)
        d_k = jnp.einsum("hqk,qhe->khe", d_scores, q_part, preferred_element_type=f32)
        d_q = d_q * HEAD ** (-0.5)
        d_k = d_k * HEAD ** (-0.5)
        return (d_q.astype(bf16), d_k.astype(bf16), d_v.astype(bf16))

    d_qs, d_ks, d_vs = lax.map(
        attend_back,
        (
            split_heads(query),
            split_heads(keys),
            split_heads(values),
            logsum,
            split_heads(d_attended),
        ),
    )
    return join_heads(d_qs), join_heads(d_ks), join_heads(d_vs)


class Links:
    def __init__(self):
        self.count = lax.axis_size("narrow")
        self.wide = lax.axis_size("wide")
        self.x = lax.axis_index("narrow")
        spot = lax.axis_index("wide")
        self.core = spot % 2
        self.y = (spot // 2) % 2
        self.z = spot // 4
        self.depth = self.wide // 4
        self.direct = self.count == 2 and self.wide == 16

    def table(self, move):
        pairs = []
        for i in range(self.count * self.wide):
            x = i % self.count
            spot = i // self.count
            to = move(x, (spot // 2) % 2, spot // 4, spot % 2)
            if to is not None:
                pairs.append((i, ((to[2] * 2 + to[1]) * 2 + to[3]) * self.count + to[0]))
        return pairs

    def send(self, value, move):
        return lax.ppermute(value, AXES, self.table(move))

    def over_x(self, value):
        return self.send(value, lambda x, y, z, c: (1 - x, y, z, c))

    def over_y(self, value):
        return self.send(value, lambda x, y, z, c: (x, 1 - y, z, c))

    def over_core(self, value):
        return self.send(value, lambda x, y, z, c: (x, y, z, 1 - c))


def pick(which, zero, one):
    return jnp.where(which == 0, zero, one)


def gather_other(links, shard):
    rows, columns = shard.shape
    tiles = rows // 8
    span = -(-tiles // 4)
    starts = [tiles * k // 4 for k in range(4)]
    view = shard.reshape(tiles, 8, columns)
    start_of = jnp.array(starts, jnp.int32)
    mine = links.y * 2 + links.core

    def at(y, core):
        return start_of[y * 2 + core]

    piece = lax.dynamic_slice_in_dim(view, start_of[mine], span, 0)
    first = links.over_x(piece)
    second = links.over_y(first)
    third = links.over_core(first)
    fourth = links.over_core(second)
    whole = jnp.zeros((tiles, 8, columns), shard.dtype)
    y, core = links.y, links.core
    for value, spot in (
        (first, at(y, core)),
        (second, at(1 - y, core)),
        (third, at(y, 1 - core)),
        (fourth, at(1 - y, 1 - core)),
    ):
        whole = lax.dynamic_update_slice_in_dim(whole, value, spot, 0)
    return whole.reshape(rows, columns)


class Weight:
    def __init__(self, links, shard):
        self.links = links
        self.own = shard
        if links.direct:
            self.other = gather_other(links, shard)
        else:
            self.full = lax.all_gather(shard, "narrow", axis=0, tiled=True)

    def apply(self, left):
        if not self.links.direct:
            return dot(left, self.full)
        x = self.links.x
        half = left.shape[1] // 2
        mine = pick(x, left[:, :half], left[:, half:])
        theirs = pick(x, left[:, half:], left[:, :half])
        return dot(mine, self.own) + dot(theirs, self.other)

    def apply_t(self, left):
        if not self.links.direct:
            return dot_t(left, self.full)
        x = self.links.x
        mine = dot_t(left, self.own)
        theirs = dot_t(left, self.other)
        return jnp.concatenate([pick(x, mine, theirs), pick(x, theirs, mine)], axis=1)


def weight_grad(links, left, right):
    if not links.direct:
        grad = tdot(left, right).astype(bf16)
        grad = lax.psum_scatter(grad, "narrow", scatter_dimension=0, tiled=True)
        return lax.psum_scatter(grad, "wide", scatter_dimension=1, tiled=True).astype(f32)
    x, y, z, core = links.x, links.y, links.z, links.core
    rows, columns = left.shape[1], right.shape[1]
    half = rows // 2
    unit = columns // 8
    right_own = pick(core, right[:, : columns // 2], right[:, columns // 2 :])
    right_away = pick(core, right[:, columns // 2 :], right[:, : columns // 2])
    right_all = jnp.concatenate([right_own, links.over_core(right_away)], axis=0)
    left_all = jnp.concatenate([left, links.over_core(left)], axis=0)
    left_own = pick(x, left_all[:, :half], left_all[:, half:])
    left_away = pick(x, left_all[:, half:], left_all[:, :half])
    cut = [right_all[:, k * unit : (k + 1) * unit] for k in range(4)]
    near = [pick(y, cut[0], cut[1]), pick(y, cut[2], cut[3])]
    far = [pick(y, cut[1], cut[0]), pick(y, cut[3], cut[2])]

    def both(one, two):
        return jnp.stack([one.astype(bf16), two.astype(bf16)])

    got_x = links.over_x(both(tdot(far[0], left_away), tdot(near[0], left_away)))
    got_y = links.over_y(both(tdot(far[1], left_away), tdot(far[1], left_own)))
    sum_far = tdot(far[0], left_own) + got_x[0].astype(f32)
    even = tdot(near[0], left_own) + got_x[1].astype(f32)
    sum_away = tdot(near[1], left_away) + got_y[0].astype(f32)
    odd = tdot(near[1], left_own) + got_y[1].astype(f32)
    even = even + links.over_y(sum_far.astype(bf16)).astype(f32)
    odd = odd + links.over_x(sum_away.astype(bf16)).astype(f32)
    low = z % 2 == 0
    even_b, odd_b = even.astype(bf16), odd.astype(bf16)
    same = jnp.where(low, odd_b, even_b)
    straight = jnp.where(low, even_b, odd_b)
    got_1 = links.send(same, lambda x, y, z, c: (x, y, z ^ 1, c) if z // 2 == c else None)
    got_2 = links.send(straight, lambda x, y, z, c: (x, y, z ^ 2, c) if z // 2 != c else None)
    got_3 = links.send(same, lambda x, y, z, c: (x, y, z ^ 3, c) if z // 2 != c else None)
    total = jnp.where(low, even, odd)
    total = total + got_1.astype(f32) + got_2.astype(f32) + got_3.astype(f32)
    part = unit // 2
    zero_part, one_part = total[:part], total[part:]
    got = links.send(
        pick(core, one_part, zero_part),
        lambda x, y, z, c: (x, y, z, 1 - c) if z // 2 == c else None,
    )
    result = jnp.where(z // 2 == core, pick(core, zero_part, one_part), got)
    return result.T


def gather_vectors(links, vectors):
    lengths = [v.shape[0] for v in vectors]
    if not links.direct:
        return [lax.all_gather(v, "narrow", axis=0, tiled=True).astype(f32) for v in vectors]
    packed = jnp.concatenate(vectors)
    other = links.over_x(packed)
    full = []
    at = 0
    for length in lengths:
        mine, theirs = packed[at : at + length], other[at : at + length]
        joined = jnp.concatenate([pick(links.x, mine, theirs), pick(links.x, theirs, mine)])
        full.append(joined.astype(f32))
        at += length
    return full


def vector_grads(links, sums):
    lengths = [v.shape[0] for v in sums]
    total = lax.psum(jnp.concatenate(sums), AXES)
    parts = []
    at = 0
    for length in lengths:
        own = length // links.count
        parts.append(lax.dynamic_slice_in_dim(total, at + links.x * own, own, 0))
        at += length
    return parts


def local(
    tokens,
    lengths,
    dropped,
    cotangent,
    first_gain,
    first_shift,
    qkv_weight,
    query_bias,
    value_bias,
    out_weight,
    out_bias,
    second_gain,
    second_shift,
    up_weight,
    up_bias,
    down_weight,
    down_bias,
):
    links = Links()
    rows, width = tokens.shape[1:]
    mask = key_mask(lengths[0], dropped[0], rows)
    inputs = tokens[0].astype(f32)
    grad_out = cotangent[0]
    (gain1, shift1, q_bias, v_bias, o_bias, gain2, shift2, d_bias, u_bias) = gather_vectors(
        links,
        [
            first_gain,
            first_shift,
            query_bias,
            value_bias,
            out_bias,
            second_gain,
            second_shift,
            down_bias,
            up_bias,
        ],
    )
    w_qkv = Weight(links, qkv_weight)
    w_out = Weight(links, out_weight)
    w_up = Weight(links, up_weight)
    w_down = Weight(links, down_weight)

    first = normed(inputs, gain1, shift1).astype(bf16)
    mixed = w_qkv.apply(first)
    query = (mixed[:, :width] + q_bias).astype(bf16)
    keys = mixed[:, width : 2 * width].astype(bf16)
    values = (mixed[:, 2 * width :] + v_bias).astype(bf16)
    attended, logsum = attention(query, keys, values, mask)
    middle = inputs + (w_out.apply(attended) + o_bias)
    second = normed(middle, gain2, shift2).astype(bf16)
    hidden = w_up.apply(second) + u_bias
    active = jax.nn.gelu(hidden, approximate=True).astype(bf16)
    g_down = weight_grad(links, active, grad_out)
    result = middle + (w_down.apply(active) + d_bias)
    output = result.astype(bf16)[None]

    d_active = w_down.apply_t(grad_out)
    unused, gelu_pull = jax.vjp(lambda v: jax.nn.gelu(v, approximate=True), hidden)
    d_hidden = gelu_pull(d_active)[0].astype(bf16)
    g_up = weight_grad(links, second, d_hidden)
    d_second = w_up.apply_t(d_hidden)
    unused, norm_pull = jax.vjp(normed, middle, gain2, shift2)
    d_middle, d_gain2, d_shift2 = norm_pull(d_second)
    d_middle = d_middle + grad_out.astype(f32)
    d_branch = d_middle.astype(bf16)
    g_out = weight_grad(links, attended, d_branch)
    d_attended = w_out.apply_t(d_branch).astype(bf16)
    d_query, d_keys, d_values = attention_back(query, keys, values, logsum, d_attended, mask)
    d_mixed = jnp.concatenate([d_query, d_keys, d_values], axis=1)
    g_qkv = weight_grad(links, first, d_mixed)
    d_first = w_qkv.apply_t(d_mixed)
    unused, first_pull = jax.vjp(normed, inputs, gain1, shift1)
    d_inputs, d_gain1, d_shift1 = first_pull(d_first)
    grad_tokens = (d_middle + d_inputs)[None]

    def column_sum(values):
        return jnp.sum(values.astype(f32), axis=0)

    v_gain1, v_shift1, v_q, v_v, v_o, v_gain2, v_shift2, v_up, v_down = vector_grads(
        links,
        [
            d_gain1,
            d_shift1,
            column_sum(d_query),
            column_sum(d_values),
            column_sum(d_branch),
            d_gain2,
            d_shift2,
            column_sum(d_hidden),
            column_sum(grad_out),
        ],
    )
    return (
        output,
        grad_tokens,
        v_gain1,
        v_shift1,
        g_qkv,
        v_q,
        v_v,
        g_out,
        v_o,
        v_gain2,
        v_shift2,
        g_up,
        v_up,
        g_down,
        v_down,
    )


def solution(mesh):
    batch = P(AXES, None, None)
    vector = P("narrow")
    matrix = P("narrow", None)
    return jax.shard_map(
        local,
        mesh=mesh,
        in_specs=(
            batch,
            P(AXES),
            P(AXES),
            batch,
            vector,
            vector,
            matrix,
            vector,
            vector,
            matrix,
            vector,
            vector,
            vector,
            matrix,
            vector,
            matrix,
            vector,
        ),
        out_specs=(
            batch,
            batch,
            vector,
            vector,
            P("narrow", "wide"),
            vector,
            vector,
            P("narrow", "wide"),
            vector,
            vector,
            vector,
            P("narrow", "wide"),
            vector,
            P("narrow", "wide"),
            vector,
        ),
        check_vma=False,
    )
```

time: 1120 us -> 580 us (0.52)
  waiting for transfers between devices: 840 us -> 260 us
  starting transfers between devices: 0.97 us -> 58.2 us
  local copies, waits for them, and re-layouts: 16.4 us -> 58.6 us
  blocking collectives: 81.9 us -> 40.1 us
  matrix products: 134 us -> 97.7 us
  other arithmetic: 16.3 us -> 43 us
    all_gather x4 -> x0, waiting for transfers between devices: 353 us -> none  [the longest x1 123 us: local(): lax.all_gather(up_weight, 'narrow', axis=0, tiled=True)]
    unnamed x11 -> x0, waiting for transfers between devices: 295 us -> none
    ppermute x0 -> x57, waiting for transfers between devices: none -> 260 us  [send(): return lax.ppermute(value, AXES, self.table(move))]
    reduce_scatter x3 -> x0, waiting for transfers between devices: 192 us -> none  [the longest x1 123 us: local(): lax.psum_scatter(d_down.astype(jnp.bfloat16), 'narrow', scatter_dimension...]
    ppermute x0 -> x57, starting transfers between devices: none -> 58.2 us  [send(): return lax.ppermute(value, AXES, self.table(move))]
    dot_general x45 -> x76, matrix products: 129 us -> 97.7 us  [the longest x8 31.5 us: dot(): return jnp.dot(left, right, preferred_element_type=f32)]
    psum x1, blocking collectives: 64.2 us -> 40.1 us  [vector_grads(): total = lax.psum(jnp.concatenate(sums), AXES)]
    unnamed x2 -> x0, blocking collectives: 17.6 us -> none
  transfers between devices with their start and end apart: 9 -> 57, of which waited for: 8 -> 22; matrix products, arithmetic and copies ran while one was open for 12% -> 24% of each run, Pallas kernels for 0% -> 0%
where the time goes in v1:
time: 580 us; the launch traced here: 569 us
  waiting for transfers between devices  260 us (45%)
  matrix products  97.7 us (17%)
  local copies, waits for them, and re-layouts  58.6 us (10%)
  starting transfers between devices  58.2 us (10%)
  other arithmetic  43 us (7%)
  blocking collectives  40.1 us (7%)
  between operations  11.9 us (2%)
    ppermute x57, waiting for transfers between devices, send(): return lax.ppermute(value, AXES, self.table(move))  260 us
    ppermute x57, starting transfers between devices, send(): return lax.ppermute(value, AXES, self.table(move))  58.2 us
    psum x1, blocking collectives, vector_grads(): total = lax.psum(jnp.concatenate(sums), AXES)  40.1 us
    dot_general x8, matrix products, dot(): return jnp.dot(left, right, preferred_element_type=f32)  31.5 us
    dot_general x8, matrix products, dot_t(): lax.dot_general(left, right, (((1,), (1,)), ((), ())), preferred_element_...  20.1 us
    dot_general x32, matrix products, tdot(): lax.dot_general(left, right, (((0,), (0,)), ((), ())), preferred_element_...  17.8 us
    select_n x15, other arithmetic, pick(): return jnp.where(which == 0, zero, one)  16.4 us
    dynamic_update_slice x16, local copies, waits for them, and re-layouts, gather_other(): whole = lax.dynamic_update_slice_in_dim(whole, value, spot, 0)  13.5 us
  transfers between devices with their start and end apart: 57, of which 22 were waited for; matrix products, arithmetic and copies ran while one was open for 24% of the time, Pallas kernels for 0%

profile of v1, /device:TPU:0, one launch (start us, length us, event | category | flops | bytes accessed | tf_op | source)
XLA Modules:
  0.0 569.2 jit_solution(4175647565305170686)
XLA Ops:
  4.1 2.5 constant_dynamic-slice_fusion.1
  6.6 3.0 collective-permute-start.9
  10.4 2.3 constant_dynamic-slice_fusion.3
  16.8 5.7 fusion.200
  22.5 2.5 constant_dynamic-slice_fusion
  30.9 35.9 %collective-permute-done = bf16[6720]{0:T(1024)(128)(2,1)S(1)} collective-permute-done((bf16[6720]{0:T(1024)(128)(2,1)S(1)}, bf16[6720]{0:T(1024)(128)(2,1)S(1)}, u32[]{:S(2)}, u32[]{:S(2)}) %collective-permute-start) | collective-permute-done | bytes 13472 | tf_op jit(solution)/shard_map/ppermute | solution.py:122
  67.5 4.1 fusion.169
  79.7 6.2 %collective-permute-done.6 = bf16[18,8,1120]{2,1,0:T(8,128)(2,1)S(1)} collective-permute-done((bf16[18,8,1120]{2,1,0:T(8,128)(2,1)}, bf16[18,8,1120]{2,1,0:T(8,128)(2,1)S(1)}, u32[]{:S(2)}, u32[]{:S(2)}) %collective-permute-start.6) | collective-permute-done | bytes 322592 | tf_op jit(solution)/shard_map/ppermute | solution.py:122
  89.5 14.6 %collective-permute-done.13 = bf16[70,8,1120]{2,1,0:T(8,128)(2,1)S(1)} collective-permute-done((bf16[70,8,1120]{2,1,0:T(8,128)(2,1)S(1)}, bf16[70,8,1120]{2,1,0:T(8,128)(2,1)S(1)}, u32[]{:S(2)}, u32[]{:S(2)}) %collective-permute-start.13) | collective-permute-done | bytes 1254432 | tf_op jit(solution)/shard_map/ppermute | solution.py:122
  108.6 2.6 collective-permute-done.2
  112.0 26.9 %collective-permute-done.14 = bf16[70,8,1120]{2,1,0:T(8,128)(2,1)} collective-permute-done((bf16[70,8,1120]{2,1,0:T(8,128)(2,1)S(1)}, bf16[70,8,1120]{2,1,0:T(8,128)(2,1)}, u32[]{:S(2)}, u32[]{:S(2)}) %collective-permute-start.14) | collective-permute-done | bytes 1254432 | tf_op jit(solution)/shard_map/ppermute | solution.py:122
  140.7 25.5 %collective-permute-done.10 = bf16[18,8,4480]{2,1,0:T(8,128)(2,1)} collective-permute-done((bf16[18,8,4480]{2,1,0:T(8,128)(2,1)}, bf16[18,8,4480]{2,1,0:T(8,128)(2,1)}, u32[]{:S(2)}, u32[]{:S(2)}) %collective-permute-start.10) | collective-permute-done | bytes 1290272 | tf_op jit(solution)/shard_map/ppermute | solution.py:122
  167.7 2.3 copy-done.24
  174.3 10.6 %while.28 = (s32[]{:T(128)}, bf16[4,256,5,56]{1,3,2,0:T(8,128)(2,1)}, f32[4,5,256,1]{2,1,3,0:T(8,128)S(1)}, bf16[4,256,5,56]{1,3,2,0:T(8,128)(2,1)}, bf16[4,256,...) while((s32[]{:T(128)}, ...), condition=%wide.region_5.6_spmd.clone, body=%wide.region_2.5_spmd.clone.sunk | while | flops 76354304 | bytes 4689241 | solution.py:64
  188.0 2.4 fusion.213
  191.5 2.7 constant_dynamic-update-slice_fusion.5
  194.2 2.0 fusion.163
  197.5 2.5 broadcast_select_fusion.18
  205.6 7.3 %convert_reduce_fusion = (f32[4480]{0:T(1024)S(1)}, bf16[256,4480]{1,0:T(8,128)(2,1)S(1)}, bf16[256,4480]{1,0:T(8,128)(2,1)}) fusion(f32[256,2240]{1,0:T(8,128)S(1)} %get-tuple-element.203, f32[256,2240]{1,0:T(8,128)S(1)} %get-tuple-element.202, f32[4480]{0:T(1024)S(1)} %copy-done.35, f32[256,4480]{1,0:T(8,128)S(1)} %fusion.163, ...), kind=kOutput, calls=%fused_computation.88 | convolution fusion | flops 1315610240 | bytes 19389440 | tf_op jit(solution)/shard_map/dot_general | solution.py:15
  225.5 22.2 %while.29 = (s32[]{:T(128)}, bf16[4,256,5,56]{1,3,2,0:T(8,128)(2,1)}, bf16[4,256,5,56]{1,3,2,0:T(8,128)(2,1)}, bf16[4,256,5,56]{1,3,2,0:T(8,128)(2,1)}, bf16[4,2...) while((s32[]{:T(128)}, ...), condition=%wide.region_12.13_spmd.clone, body=%wide.region_10.12_spmd.clone.sunk | while | flops 187069184 | bytes 13723021 | solution.py:86
  247.7 3.0 broadcast_select_fusion.6
  250.7 4.4 fusion.150
  255.6 6.7 %fusion.128 = f32[256,1120]{0,1:T(8,128)} fusion(bf16[2240,1120]{1,0:T(8,128)(2,1)} %param.40, pred[]{:T(512)S(6)} %eq.19, bf16[256,4480]{1,0:T(8,128)(2,1)} %get-tuple-element.206), kind=kOutput, calls=%fused_computation.196 | convolution fusion | flops 1285079040 | bytes 8667137 | tf_op jit(solution)/shard_map/dot_general | solution.py:15
  262.3 2.8 copy.63
  265.8 4.1 broadcast_select_fusion.33
  272.9 5.0 fusion.95
  280.9 40.1 %psum.7 = f32[13440]{0:T(1024)S(1)} all-reduce(f32[13440]{0:T(1024)S(1)} %concatenate.137), channel_id=1, replica_groups=mesh['wide'=16,'narrow'=2] {'wide','narrow'}, use_global_device_ids=true, to_apply=%region_24.25 | all-reduce | flops 13440 | bytes 107520 | tf_op jit(solution)/shard_map/psum | solution.py:261
  323.5 2.3 collective-permute-start.31
  328.8 4.7 collective-permute-done.31
  337.2 2.6 collective-permute-done.32
  340.2 2.6 collective-permute-done.30
  343.1 3.4 collective-permute-start.33
  361.5 2.4 copy.64
  363.9 2.7 fusion.151
  368.4 2.2 collective-permute-start.39
  371.5 10.8 %collective-permute-done.21 = bf16[2,420,560]{2,0,1:T(2,128)(2,1)} collective-permute-done((bf16[2,420,560]{2,0,1:T(2,128)(2,1)}, bf16[2,420,560]{2,0,1:T(2,128)(2,1)}, u32[]{:S(2)}, u32[]{:S(2)}) %collective-permute-start.21) | collective-permute-done | bytes 940832 | tf_op jit(solution)/shard_map/ppermute | solution.py:122
  382.3 3.3 fusion.209
  387.9 3.5 fusion.210
  395.2 29.3 %collective-permute-done.22 = bf16[420,560]{1,0:T(8,128)(2,1)S(1)} collective-permute-done((bf16[420,560]{1,0:T(8,128)(2,1)S(1)}, bf16[420,560]{1,0:T(8,128)(2,1)S(1)}, u32[]{:S(2)}, u32[]{:S(2)}) %collective-permute-start.22) | collective-permute-done | bytes 470432 | tf_op jit(solution)/shard_map/ppermute | solution.py:122
  425.6 2.5 collective-permute-start.23
  430.9 4.6 broadcast_select_fusion
  445.3 12.5 %collective-permute-done.24 = bf16[420,560]{1,0:T(8,128)(2,1)S(1)} collective-permute-done((bf16[420,560]{1,0:T(8,128)(2,1)S(1)}, bf16[420,560]{1,0:T(8,128)(2,1)S(1)}, u32[]{:S(2)}, u32[]{:S(2)}) %collective-permute-start.24) | collective-permute-done | bytes 470432 | tf_op jit(solution)/shard_map/ppermute | solution.py:122
  461.1 10.1 %collective-permute-done.51 = bf16[2,140,2240]{2,0,1:T(2,128)(2,1)S(1)} collective-permute-done((bf16[2,140,2240]{2,0,1:T(2,128)(2,1)S(1)}, bf16[2,140,2240]{2,0,1:T(2,128)(2,1)S(1)}, u32[]{:S(2)}, u32[]{:S(2)}) %collective-permute-start.51) | collective-permute-done | bytes 1254432 | tf_op jit(solution)/shard_map/ppermute | solution.py:122
  473.8 15.1 %collective-permute-done.49 = bf16[2,140,2240]{2,0,1:T(2,128)(2,1)S(1)} collective-permute-done((bf16[2,140,2240]{2,0,1:T(2,128)(2,1)S(1)}, bf16[2,140,2240]{2,0,1:T(2,128)(2,1)S(1)}, u32[]{:S(2)}, u32[]{:S(2)}) %collective-permute-start.49) | collective-permute-done | bytes 1254432 | tf_op jit(solution)/shard_map/ppermute | solution.py:122
  499.2 2.8 collective-permute-done.50
  504.0 9.6 %collective-permute-done.43 = bf16[560,560]{1,0:T(8,128)(2,1)S(1)} collective-permute-done((bf16[560,560]{1,0:T(8,128)(2,1)S(1)}, bf16[560,560]{1,0:T(8,128)(2,1)S(1)}, u32[]{:S(2)}, u32[]{:S(2)}) %collective-permute-start.43) | collective-permute-done | bytes 627232 | tf_op jit(solution)/shard_map/ppermute | solution.py:122
  515.5 16.9 %collective-permute-done.44 = bf16[560,560]{1,0:T(8,128)(2,1)S(1)} collective-permute-done((bf16[560,560]{1,0:T(8,128)(2,1)S(1)}, bf16[560,560]{1,0:T(8,128)(2,1)S(1)}, u32[]{:S(2)}, u32[]{:S(2)}) %collective-permute-start.44) | collective-permute-done | bytes 627232 | tf_op jit(solution)/shard_map/ppermute | solution.py:122
  536.9 26.2 %collective-permute-done.54 = bf16[140,2240]{1,0:T(8,128)(2,1)S(1)} collective-permute-done((bf16[140,2240]{1,0:T(8,128)(2,1)S(1)}, bf16[140,2240]{1,0:T(8,128)(2,1)S(1)}, u32[]{:S(2)}, u32[]{:S(2)}) %collective-permute-start.54) | collective-permute-done | bytes 627232 | tf_op jit(solution)/shard_map/ppermute | solution.py:122
  (412 shorter events, 169.9 us)
Async XLA Ops:
  6.6 99.9 %collective-permute-start.9 = (bf16[18,8,4480]{2,1,0:T(8,128)(2,1)}, bf16[18,8,4480]{2,1,0:T(8,128)(2,1)}, u32[]{:S(2)}, u32[]{:S(2)}) collective-permute-start(bf16[18,8,4480]{2,1,0:T(8,128)(2,1)} %constant_dynamic-slice_fusion.1), channel_id=1, source_target_pairs={{0,1},{1,0},{2,3},{3,2},{4,5},{5,4},{6,7},{7,6},{8,9},{9,8},{10,11... | collective-permute-start | bytes 3870728 | tf_op jit(solution)/shard_map/ppermute | solution.py:122
  10.4 65.4 %collective-permute-start.5 = (bf16[18,8,1120]{2,1,0:T(8,128)(2,1)}, bf16[18,8,1120]{2,1,0:T(8,128)(2,1)}, u32[]{:S(2)}, u32[]{:S(2)}) collective-permute-start(bf16[18,8,1120]{2,1,0:T(8,128)(2,1)} %constant_dynamic-slice_fusion.2), channel_id=1, source_target_pairs={{0,1},{1,0},{2,3},{3,2},{4,5},{5,4},{6,7},{7,6},{8,9},{9,8},{10,11... | collective-permute-start | bytes 967688 | tf_op jit(solution)/shard_map/ppermute | solution.py:122
  12.7 73.3 %collective-permute-start.1 = (bf16[18,8,3360]{2,1,0:T(8,128)(2,1)}, bf16[18,8,3360]{2,1,0:T(8,128)(2,1)}, u32[]{:S(2)}, u32[]{:S(2)}) collective-permute-start(bf16[18,8,3360]{2,1,0:T(8,128)(2,1)} %constant_dynamic-slice_fusion.3), channel_id=1, source_target_pairs={{0,1},{1,0},{2,3},{3,2},{4,5},{5,4},{6,7},{7,6},{8,9},{9,8},{10,11... | collective-permute-start | bytes 2903048 | tf_op jit(solution)/shard_map/ppermute | solution.py:122
  14.9 52.0 %collective-permute-start = (bf16[6720]{0:T(1024)(128)(2,1)S(1)}, bf16[6720]{0:T(1024)(128)(2,1)S(1)}, u32[]{:S(2)}, u32[]{:S(2)}) collective-permute-start(bf16[6720]{0:T(1024)(128)(2,1)S(1)} %concatenate.120), channel_id=1, source_target_pairs={{0,1},{1,0},{2,3},{3,2},{4,5},{5,4},{6,7},{7,6},{8,9},{9,8},{10,11... | collective-permute-start | bytes 40328 | tf_op jit(solution)/shard_map/ppermute | solution.py:122
  15.0 58.3 %collective-permute-start.47 = (bf16[256,560]{0,1:T(8,128)(2,1)S(1)}, bf16[256,560]{0,1:T(8,128)(2,1)S(1)}, u32[]{:S(2)}, u32[]{:S(2)}) collective-permute-start(bf16[256,560]{0,1:T(8,128)(2,1)S(1)} %get-tuple-element.251), channel_id=1, source_target_pairs={{0,2},{1,3},{2,0},{3,1},{4,6},{5,7},{6,4},{7,5},{8,10},{9,11},{10,... | collective-permute-start | bytes 860168 | tf_op jit(solution)/shard_map/ppermute | solution.py:122
  73.3 30.7 %collective-permute-start.13 = (bf16[70,8,1120]{2,1,0:T(8,128)(2,1)S(1)}, bf16[70,8,1120]{2,1,0:T(8,128)(2,1)S(1)}, u32[]{:S(2)}, u32[]{:S(2)}) collective-permute-start(bf16[70,8,1120]{2,1,0:T(8,128)(2,1)S(1)} %copy-done.30), channel_id=1, source_target_pairs={{0,1},{1,0},{2,3},{3,2},{4,5},{5,4},{6,7},{7,6},{8,9},{9,8},{10,11... | collective-permute-start | bytes 3763208 | tf_op jit(solution)/shard_map/ppermute | solution.py:122
  75.8 10.1 %collective-permute-start.6 = (bf16[18,8,1120]{2,1,0:T(8,128)(2,1)}, bf16[18,8,1120]{2,1,0:T(8,128)(2,1)S(1)}, u32[]{:S(2)}, u32[]{:S(2)}) collective-permute-start(bf16[18,8,1120]{2,1,0:T(8,128)(2,1)} %collective-permute-done.5), channel_id=1, source_target_pairs={{0,4},{1,5},{2,6},{3,7},{4,0},{5,1},{6,2},{7,3},{8,12},{9,13},{10,... | collective-permute-start | bytes 967688 | tf_op jit(solution)/shard_map/ppermute | solution.py:122
  86.0 25.2 %collective-permute-start.2 = (bf16[18,8,3360]{2,1,0:T(8,128)(2,1)}, bf16[18,8,3360]{2,1,0:T(8,128)(2,1)S(1)}, u32[]{:S(2)}, u32[]{:S(2)}) collective-permute-start(bf16[18,8,3360]{2,1,0:T(8,128)(2,1)} %collective-permute-done.1), channel_id=1, source_target_pairs={{0,4},{1,5},{2,6},{3,7},{4,0},{5,1},{6,2},{7,3},{8,12},{9,13},{10,... | collective-permute-start | bytes 2903048 | tf_op jit(solution)/shard_map/ppermute | solution.py:122
  87.6 23.7 %collective-permute-start.3 = (bf16[18,8,3360]{2,1,0:T(8,128)(2,1)}, bf16[18,8,3360]{2,1,0:T(8,128)(2,1)S(1)}, u32[]{:S(2)}, u32[]{:S(2)}) collective-permute-start(bf16[18,8,3360]{2,1,0:T(8,128)(2,1)} %collective-permute-done.1), channel_id=1, source_target_pairs={{0,2},{1,3},{2,0},{3,1},{4,6},{5,7},{6,4},{7,5},{8,10},{9,11},{10,... | collective-permute-start | bytes 2903048 | tf_op jit(solution)/shard_map/ppermute | solution.py:122
  104.1 34.9 %collective-permute-start.14 = (bf16[70,8,1120]{2,1,0:T(8,128)(2,1)S(1)}, bf16[70,8,1120]{2,1,0:T(8,128)(2,1)}, u32[]{:S(2)}, u32[]{:S(2)}) collective-permute-start(bf16[70,8,1120]{2,1,0:T(8,128)(2,1)S(1)} %collective-permute-done.13), channel_id=1, source_target_pairs={{0,4},{1,5},{2,6},{3,7},{4,0},{5,1},{6,2},{7,3},{8,12},{9,13},{10,... | collective-permute-start | bytes 3763208 | tf_op jit(solution)/shard_map/ppermute | solution.py:122
  105.8 34.6 %collective-permute-start.15 = (bf16[70,8,1120]{2,1,0:T(8,128)(2,1)S(1)}, bf16[70,8,1120]{2,1,0:T(8,128)(2,1)S(1)}, u32[]{:S(2)}, u32[]{:S(2)}) collective-permute-start(bf16[70,8,1120]{2,1,0:T(8,128)(2,1)S(1)} %collective-permute-done.13), channel_id=1, source_target_pairs={{0,2},{1,3},{2,0},{3,1},{4,6},{5,7},{6,4},{7,5},{8,10},{9,11},{10,... | collective-permute-start | bytes 3763208 | tf_op jit(solution)/shard_map/ppermute | solution.py:122
  106.4 59.7 %collective-permute-start.10 = (bf16[18,8,4480]{2,1,0:T(8,128)(2,1)}, bf16[18,8,4480]{2,1,0:T(8,128)(2,1)}, u32[]{:S(2)}, u32[]{:S(2)}) collective-permute-start(bf16[18,8,4480]{2,1,0:T(8,128)(2,1)} %collective-permute-done.9), channel_id=1, source_target_pairs={{0,4},{1,5},{2,6},{3,7},{4,0},{5,1},{6,2},{7,3},{8,12},{9,13},{10,... | collective-permute-start | bytes 3870728 | tf_op jit(solution)/shard_map/ppermute | solution.py:122
  111.2 80.3 %collective-permute-start.11 = (bf16[18,8,4480]{2,1,0:T(8,128)(2,1)}, bf16[18,8,4480]{2,1,0:T(8,128)(2,1)}, u32[]{:S(2)}, u32[]{:S(2)}) collective-permute-start(bf16[18,8,4480]{2,1,0:T(8,128)(2,1)} %collective-permute-done.9), channel_id=1, source_target_pairs={{0,2},{1,3},{2,0},{3,1},{4,6},{5,7},{6,4},{7,5},{8,10},{9,11},{10,... | collective-permute-start | bytes 3870728 | tf_op jit(solution)/shard_map/ppermute | solution.py:122
  111.3 56.3 %collective-permute-start.4 = (bf16[18,8,3360]{2,1,0:T(8,128)(2,1)S(1)}, bf16[18,8,3360]{2,1,0:T(8,128)(2,1)S(1)}, u32[]{:S(2)}, u32[]{:S(2)}) collective-permute-start(bf16[18,8,3360]{2,1,0:T(8,128)(2,1)S(1)} %collective-permute-done.2), channel_id=1, source_target_pairs={{0,2},{1,3},{2,0},{3,1},{4,6},{5,7},{6,4},{7,5},{8,10},{9,11},{10,... | collective-permute-start | bytes 2903048 | tf_op jit(solution)/shard_map/ppermute | solution.py:122
  139.0 61.1 %collective-permute-start.16 = (bf16[70,8,1120]{2,1,0:T(8,128)(2,1)}, bf16[70,8,1120]{2,1,0:T(8,128)(2,1)}, u32[]{:S(2)}, u32[]{:S(2)}) collective-permute-start(bf16[70,8,1120]{2,1,0:T(8,128)(2,1)} %collective-permute-done.14), channel_id=1, source_target_pairs={{0,2},{1,3},{2,0},{3,1},{4,6},{5,7},{6,4},{7,5},{8,10},{9,11},{10,... | collective-permute-start | bytes 3763208 | tf_op jit(solution)/shard_map/ppermute | solution.py:122
  166.2 37.9 %collective-permute-start.12 = (bf16[18,8,4480]{2,1,0:T(8,128)(2,1)}, bf16[18,8,4480]{2,1,0:T(8,128)(2,1)}, u32[]{:S(2)}, u32[]{:S(2)}) collective-permute-start(bf16[18,8,4480]{2,1,0:T(8,128)(2,1)} %collective-permute-done.10), channel_id=1, source_target_pairs={{0,2},{1,3},{2,0},{3,1},{4,6},{5,7},{6,4},{7,5},{8,10},{9,11},{10,... | collective-permute-start | bytes 3870728 | tf_op jit(solution)/shard_map/ppermute | solution.py:122
  255.1 174.3 %collective-permute-start.48 = (bf16[256,4480]{1,0:T(8,128)(2,1)}, bf16[256,4480]{1,0:T(8,128)(2,1)}, u32[]{:S(2)}, u32[]{:S(2)}) collective-permute-start(bf16[256,4480]{1,0:T(8,128)(2,1)} %get-tuple-element.206), channel_id=1, source_target_pairs={{0,2},{1,3},{2,0},{3,1},{4,6},{5,7},{6,4},{7,5},{8,10},{9,11},{10,... | collective-permute-start | bytes 6881288 | tf_op jit(solution)/shard_map/ppermute | solution.py:122
  265.1 96.4 %collective-permute-start.37 = (bf16[256,2240]{0,1:T(8,128)(2,1)}, bf16[256,2240]{0,1:T(8,128)(2,1)}, u32[]{:S(2)}, u32[]{:S(2)}) collective-permute-start(bf16[256,2240]{0,1:T(8,128)(2,1)} %copy.63), channel_id=1, source_target_pairs={{0,2},{1,3},{2,0},{3,1},{4,6},{5,7},{6,4},{7,5},{8,10},{9,11},{10,... | collective-permute-start | bytes 3440648 | tf_op jit(solution)/shard_map/ppermute | solution.py:122
  265.2 56.4 %collective-permute-start.27 = (bf16[256,560]{0,1:T(8,128)(2,1)}, bf16[256,560]{0,1:T(8,128)(2,1)}, u32[]{:S(2)}, u32[]{:S(2)}) collective-permute-start(bf16[256,560]{0,1:T(8,128)(2,1)} %get-tuple-element.257), channel_id=1, source_target_pairs={{0,2},{1,3},{2,0},{3,1},{4,6},{5,7},{6,4},{7,5},{8,10},{9,11},{10,... | collective-permute-start | bytes 860168 | tf_op jit(solution)/shard_map/ppermute | solution.py:122
  265.7 82.1 %collective-permute-start.17 = (bf16[256,1680]{0,1:T(8,128)(2,1)}, bf16[256,1680]{0,1:T(8,128)(2,1)}, u32[]{:S(2)}, u32[]{:S(2)}) collective-permute-start(bf16[256,1680]{0,1:T(8,128)(2,1)} %get-tuple-element.225), channel_id=1, source_target_pairs={{0,2},{1,3},{2,0},{3,1},{4,6},{5,7},{6,4},{7,5},{8,10},{9,11},{10,... | collective-permute-start | bytes 2580488 | tf_op jit(solution)/shard_map/ppermute | solution.py:122
  326.7 10.1 %collective-permute-start.29 = (bf16[2,140,560]{2,1,0:T(8,128)(2,1)S(1)}, bf16[2,140,560]{2,1,0:T(8,128)(2,1)S(1)}, u32[]{:S(2)}, u32[]{:S(2)}) collective-permute-start(bf16[2,140,560]{2,1,0:T(8,128)(2,1)S(1)} %pad_maximum_fusion.20), channel_id=1, source_target_pairs={{0,1},{1,0},{2,3},{3,2},{4,5},{5,4},{6,7},{7,6},{8,9},{9,8},{10,11... | collective-permute-start | bytes 940808 | tf_op jit(solution)/shard_map/ppermute | solution.py:122
  343.1 14.5 %collective-permute-start.33 = (bf16[140,560]{1,0:T(8,128)(2,1)S(1)}, bf16[140,560]{1,0:T(8,128)(2,1)S(1)}, u32[]{:S(2)}, u32[]{:S(2)}) collective-permute-start(bf16[140,560]{1,0:T(8,128)(2,1)S(1)} %get-tuple-element.246), channel_id=1, source_target_pairs={{0,8},{1,9},{4,12},{5,13},{8,0},{9,1},{12,4},{13,5},{18,26},{19,27... | collective-permute-start | bytes 470408 | tf_op jit(solution)/shard_map/ppermute | solution.py:122
  346.5 13.4 %collective-permute-start.35 = (bf16[140,560]{1,0:T(8,128)(2,1)S(1)}, bf16[140,560]{1,0:T(8,128)(2,1)S(1)}, u32[]{:S(2)}, u32[]{:S(2)}) collective-permute-start(bf16[140,560]{1,0:T(8,128)(2,1)S(1)} %get-tuple-element.246), channel_id=1, source_target_pairs={{2,26},{3,27},{6,30},{7,31},{10,18},{11,19},{14,22},{15,23},{16,8}... | collective-permute-start | bytes 470408 | tf_op jit(solution)/shard_map/ppermute | solution.py:122
  347.8 12.0 %collective-permute-start.34 = (bf16[140,560]{1,0:T(8,128)(2,1)S(1)}, bf16[140,560]{1,0:T(8,128)(2,1)S(1)}, u32[]{:S(2)}, u32[]{:S(2)}) collective-permute-start(bf16[140,560]{1,0:T(8,128)(2,1)S(1)} %get-tuple-element.245), channel_id=1, source_target_pairs={{2,18},{3,19},{6,22},{7,23},{10,26},{11,27},{14,30},{15,31},{16,0}... | collective-permute-start | bytes 470408 | tf_op jit(solution)/shard_map/ppermute | solution.py:122
  357.7 30.3 %collective-permute-start.19 = (bf16[2,420,560]{2,0,1:T(2,128)(2,1)}, bf16[2,420,560]{2,0,1:T(2,128)(2,1)}, u32[]{:S(2)}, u32[]{:S(2)}) collective-permute-start(bf16[2,420,560]{2,0,1:T(2,128)(2,1)} %copy.57), channel_id=1, source_target_pairs={{0,1},{1,0},{2,3},{3,2},{4,5},{5,4},{6,7},{7,6},{8,9},{9,8},{10,11... | collective-permute-start | bytes 2822408 | tf_op jit(solution)/shard_map/ppermute | solution.py:122
  359.8 22.4 %collective-permute-start.21 = (bf16[2,420,560]{2,0,1:T(2,128)(2,1)}, bf16[2,420,560]{2,0,1:T(2,128)(2,1)}, u32[]{:S(2)}, u32[]{:S(2)}) collective-permute-start(bf16[2,420,560]{2,0,1:T(2,128)(2,1)} %copy.60), channel_id=1, source_target_pairs={{0,4},{1,5},{2,6},{3,7},{4,0},{5,1},{6,2},{7,3},{8,12},{9,13},{10,... | collective-permute-start | bytes 2822408 | tf_op jit(solution)/shard_map/ppermute | solution.py:122
  368.4 72.9 %collective-permute-start.39 = (bf16[2,560,560]{2,1,0:T(8,128)(2,1)S(1)}, bf16[2,560,560]{2,1,0:T(8,128)(2,1)S(1)}, u32[]{:S(2)}, u32[]{:S(2)}) collective-permute-start(bf16[2,560,560]{2,1,0:T(8,128)(2,1)S(1)} %pad_maximum_fusion.3), channel_id=1, source_target_pairs={{0,1},{1,0},{2,3},{3,2},{4,5},{5,4},{6,7},{7,6},{8,9},{9,8},{10,11... | collective-permute-start | bytes 3763208 | tf_op jit(solution)/shard_map/ppermute | solution.py:122
  386.2 38.3 %collective-permute-start.22 = (bf16[420,560]{1,0:T(8,128)(2,1)S(1)}, bf16[420,560]{1,0:T(8,128)(2,1)S(1)}, u32[]{:S(2)}, u32[]{:S(2)}) collective-permute-start(bf16[420,560]{1,0:T(8,128)(2,1)S(1)} %fusion.111), channel_id=1, source_target_pairs={{0,1},{1,0},{2,3},{3,2},{4,5},{5,4},{6,7},{7,6},{8,9},{9,8},{10,11... | collective-permute-start | bytes 1411208 | tf_op jit(solution)/shard_map/ppermute | solution.py:122
  392.0 33.0 %collective-permute-start.20 = (bf16[420,560]{1,0:T(8,128)(2,1)S(1)}, bf16[420,560]{1,0:T(8,128)(2,1)S(1)}, u32[]{:S(2)}, u32[]{:S(2)}) collective-permute-start(bf16[420,560]{1,0:T(8,128)(2,1)S(1)} %fusion.110), channel_id=1, source_target_pairs={{0,4},{1,5},{2,6},{3,7},{4,0},{5,1},{6,2},{7,3},{8,12},{9,13},{10,... | collective-permute-start | bytes 1411208 | tf_op jit(solution)/shard_map/ppermute | solution.py:122
  393.7 46.2 %collective-permute-start.41 = (bf16[2,560,560]{2,1,0:T(8,128)(2,1)S(1)}, bf16[2,560,560]{2,1,0:T(8,128)(2,1)S(1)}, u32[]{:S(2)}, u32[]{:S(2)}) collective-permute-start(bf16[2,560,560]{2,1,0:T(8,128)(2,1)S(1)} %pad_maximum_fusion.4), channel_id=1, source_target_pairs={{0,4},{1,5},{2,6},{3,7},{4,0},{5,1},{6,2},{7,3},{8,12},{9,13},{10,... | collective-permute-start | bytes 3763208 | tf_op jit(solution)/shard_map/ppermute | solution.py:122
  425.6 18.1 %collective-permute-start.23 = (bf16[420,560]{1,0:T(8,128)(2,1)S(1)}, bf16[420,560]{1,0:T(8,128)(2,1)S(1)}, u32[]{:S(2)}, u32[]{:S(2)}) collective-permute-start(bf16[420,560]{1,0:T(8,128)(2,1)S(1)} %get-tuple-element.220), channel_id=1, source_target_pairs={{0,8},{1,9},{4,12},{5,13},{8,0},{9,1},{12,4},{13,5},{18,26},{19,27... | collective-permute-start | bytes 1411208 | tf_op jit(solution)/shard_map/ppermute | solution.py:122
  428.1 29.9 %collective-permute-start.25 = (bf16[420,560]{1,0:T(8,128)(2,1)S(1)}, bf16[420,560]{1,0:T(8,128)(2,1)S(1)}, u32[]{:S(2)}, u32[]{:S(2)}) collective-permute-start(bf16[420,560]{1,0:T(8,128)(2,1)S(1)} %get-tuple-element.220), channel_id=1, source_target_pairs={{2,26},{3,27},{6,30},{7,31},{10,18},{11,19},{14,22},{15,23},{16,8}... | collective-permute-start | bytes 1411208 | tf_op jit(solution)/shard_map/ppermute | solution.py:122
  429.4 28.3 %collective-permute-start.24 = (bf16[420,560]{1,0:T(8,128)(2,1)S(1)}, bf16[420,560]{1,0:T(8,128)(2,1)S(1)}, u32[]{:S(2)}, u32[]{:S(2)}) collective-permute-start(bf16[420,560]{1,0:T(8,128)(2,1)S(1)} %get-tuple-element.219), channel_id=1, source_target_pairs={{2,18},{3,19},{6,22},{7,23},{10,26},{11,27},{14,30},{15,31},{16,0}... | collective-permute-start | bytes 1411208 | tf_op jit(solution)/shard_map/ppermute | solution.py:122
  439.9 31.3 %collective-permute-start.51 = (bf16[2,140,2240]{2,0,1:T(2,128)(2,1)S(1)}, bf16[2,140,2240]{2,0,1:T(2,128)(2,1)S(1)}, u32[]{:S(2)}, u32[]{:S(2)}) collective-permute-start(bf16[2,140,2240]{2,0,1:T(2,128)(2,1)S(1)} %copy.68), channel_id=1, source_target_pairs={{0,4},{1,5},{2,6},{3,7},{4,0},{5,1},{6,2},{7,3},{8,12},{9,13},{10,... | collective-permute-start | bytes 3763208 | tf_op jit(solution)/shard_map/ppermute | solution.py:122
  441.4 19.0 %collective-permute-start.42 = (bf16[560,560]{1,0:T(8,128)(2,1)S(1)}, bf16[560,560]{1,0:T(8,128)(2,1)S(1)}, u32[]{:S(2)}, u32[]{:S(2)}) collective-permute-start(bf16[560,560]{1,0:T(8,128)(2,1)S(1)} %fusion.109), channel_id=1, source_target_pairs={{0,1},{1,0},{2,3},{3,2},{4,5},{5,4},{6,7},{7,6},{8,9},{9,8},{10,11... | collective-permute-start | bytes 1881608 | tf_op jit(solution)/shard_map/ppermute | solution.py:122
  443.7 121.4 %collective-permute-start.36 = (f32[70,560]{1,0:T(8,128)S(1)}, f32[70,560]{1,0:T(8,128)S(1)}, u32[]{:S(2)}, u32[]{:S(2)}) collective-permute-start(f32[70,560]{1,0:T(8,128)S(1)} %copy-done.33), channel_id=1, source_target_pairs={{0,2},{1,3},{4,6},{5,7},{8,10},{9,11},{12,14},{13,15},{18,16},{19,... | collective-permute-start | bytes 470408 | tf_op jit(solution)/shard_map/ppermute | solution.py:122
  457.7 31.2 %collective-permute-start.49 = (bf16[2,140,2240]{2,0,1:T(2,128)(2,1)S(1)}, bf16[2,140,2240]{2,0,1:T(2,128)(2,1)S(1)}, u32[]{:S(2)}, u32[]{:S(2)}) collective-permute-start(bf16[2,140,2240]{2,0,1:T(2,128)(2,1)S(1)} %copy.65), channel_id=1, source_target_pairs={{0,1},{1,0},{2,3},{3,2},{4,5},{5,4},{6,7},{7,6},{8,9},{9,8},{10,11... | collective-permute-start | bytes 3763208 | tf_op jit(solution)/shard_map/ppermute | solution.py:122
  458.0 33.9 %collective-permute-start.40 = (bf16[560,560]{1,0:T(8,128)(2,1)S(1)}, bf16[560,560]{1,0:T(8,128)(2,1)S(1)}, u32[]{:S(2)}, u32[]{:S(2)}) collective-permute-start(bf16[560,560]{1,0:T(8,128)(2,1)S(1)} %fusion.108), channel_id=1, source_target_pairs={{0,4},{1,5},{2,6},{3,7},{4,0},{5,1},{6,2},{7,3},{8,12},{9,13},{10,... | collective-permute-start | bytes 1881608 | tf_op jit(solution)/shard_map/ppermute | solution.py:122
  473.5 23.8 %collective-permute-start.52 = (bf16[140,2240]{1,0:T(8,128)(2,1)S(1)}, bf16[140,2240]{1,0:T(8,128)(2,1)S(1)}, u32[]{:S(2)}, u32[]{:S(2)}) collective-permute-start(bf16[140,2240]{1,0:T(8,128)(2,1)S(1)} %fusion.76), channel_id=1, source_target_pairs={{0,1},{1,0},{2,3},{3,2},{4,5},{5,4},{6,7},{7,6},{8,9},{9,8},{10,11... | collective-permute-start | bytes 1881608 | tf_op jit(solution)/shard_map/ppermute | solution.py:122
  491.2 10.7 %collective-permute-start.50 = (bf16[140,2240]{1,0:T(8,128)(2,1)S(1)}, bf16[140,2240]{1,0:T(8,128)(2,1)S(1)}, u32[]{:S(2)}, u32[]{:S(2)}) collective-permute-start(bf16[140,2240]{1,0:T(8,128)(2,1)S(1)} %fusion.75), channel_id=1, source_target_pairs={{0,4},{1,5},{2,6},{3,7},{4,0},{5,1},{6,2},{7,3},{8,12},{9,13},{10,... | collective-permute-start | bytes 1881608 | tf_op jit(solution)/shard_map/ppermute | solution.py:122
  492.7 20.8 %collective-permute-start.43 = (bf16[560,560]{1,0:T(8,128)(2,1)S(1)}, bf16[560,560]{1,0:T(8,128)(2,1)S(1)}, u32[]{:S(2)}, u32[]{:S(2)}) collective-permute-start(bf16[560,560]{1,0:T(8,128)(2,1)S(1)} %get-tuple-element.210), channel_id=1, source_target_pairs={{0,8},{1,9},{4,12},{5,13},{8,0},{9,1},{12,4},{13,5},{18,26},{19,27... | collective-permute-start | bytes 1881608 | tf_op jit(solution)/shard_map/ppermute | solution.py:122
  494.7 39.0 %collective-permute-start.45 = (bf16[560,560]{1,0:T(8,128)(2,1)S(1)}, bf16[560,560]{1,0:T(8,128)(2,1)S(1)}, u32[]{:S(2)}, u32[]{:S(2)}) collective-permute-start(bf16[560,560]{1,0:T(8,128)(2,1)S(1)} %get-tuple-element.210), channel_id=1, source_target_pairs={{2,26},{3,27},{6,30},{7,31},{10,18},{11,19},{14,22},{15,23},{16,8}... | collective-permute-start | bytes 1881608 | tf_op jit(solution)/shard_map/ppermute | solution.py:122
  497.3 35.1 %collective-permute-start.44 = (bf16[560,560]{1,0:T(8,128)(2,1)S(1)}, bf16[560,560]{1,0:T(8,128)(2,1)S(1)}, u32[]{:S(2)}, u32[]{:S(2)}) collective-permute-start(bf16[560,560]{1,0:T(8,128)(2,1)S(1)} %get-tuple-element.209), channel_id=1, source_target_pairs={{2,18},{3,19},{6,22},{7,23},{10,26},{11,27},{14,30},{15,31},{16,0}... | collective-permute-start | bytes 1881608 | tf_op jit(solution)/shard_map/ppermute | solution.py:122
  502.0 63.8 %collective-permute-start.26 = (f32[210,560]{1,0:T(8,128)S(1)}, f32[210,560]{1,0:T(8,128)S(1)}, u32[]{:S(2)}, u32[]{:S(2)}) collective-permute-start(f32[210,560]{1,0:T(8,128)S(1)} %slice_select_fusion.2), channel_id=1, source_target_pairs={{0,2},{1,3},{4,6},{5,7},{8,10},{9,11},{12,14},{13,15},{18,16},{19,... | collective-permute-start | bytes 1411208 | tf_op jit(solution)/shard_map/ppermute | solution.py:122
  513.6 22.0 %collective-permute-start.53 = (bf16[140,2240]{1,0:T(8,128)(2,1)S(1)}, bf16[140,2240]{1,0:T(8,128)(2,1)S(1)}, u32[]{:S(2)}, u32[]{:S(2)}) collective-permute-start(bf16[140,2240]{1,0:T(8,128)(2,1)S(1)} %get-tuple-element.212), channel_id=1, source_target_pairs={{0,8},{1,9},{4,12},{5,13},{8,0},{9,1},{12,4},{13,5},{18,26},{19,27... | collective-permute-start | bytes 1881608 | tf_op jit(solution)/shard_map/ppermute | solution.py:122
  532.4 30.7 %collective-permute-start.55 = (bf16[140,2240]{1,0:T(8,128)(2,1)S(1)}, bf16[140,2240]{1,0:T(8,128)(2,1)S(1)}, u32[]{:S(2)}, u32[]{:S(2)}) collective-permute-start(bf16[140,2240]{1,0:T(8,128)(2,1)S(1)} %get-tuple-element.212), channel_id=1, source_target_pairs={{2,26},{3,27},{6,30},{7,31},{10,18},{11,19},{14,22},{15,23},{16,8}... | collective-permute-start | bytes 1881608 | tf_op jit(solution)/shard_map/ppermute | solution.py:122
  533.7 29.4 %collective-permute-start.54 = (bf16[140,2240]{1,0:T(8,128)(2,1)S(1)}, bf16[140,2240]{1,0:T(8,128)(2,1)S(1)}, u32[]{:S(2)}, u32[]{:S(2)}) collective-permute-start(bf16[140,2240]{1,0:T(8,128)(2,1)S(1)} %get-tuple-element.211), channel_id=1, source_target_pairs={{2,18},{3,19},{6,22},{7,23},{10,26},{11,27},{14,30},{15,31},{16,0}... | collective-permute-start | bytes 1881608 | tf_op jit(solution)/shard_map/ppermute | solution.py:122
  535.5 31.2 %collective-permute-start.46 = (f32[280,560]{1,0:T(8,128)S(1)}, f32[280,560]{1,0:T(8,128)S(1)}, u32[]{:S(2)}, u32[]{:S(2)}) collective-permute-start(f32[280,560]{1,0:T(8,128)S(1)} %slice_select_fusion), channel_id=1, source_target_pairs={{0,2},{1,3},{4,6},{5,7},{8,10},{9,11},{12,14},{13,15},{18,16},{19,... | collective-permute-start | bytes 1881608 | tf_op jit(solution)/shard_map/ppermute | solution.py:122
  (72 other events, 484.9 us)

commit v2 on v1

--- a/solution.py
+++ b/solution.py
@@ -1,6 +1,10 @@
+import functools
+
 import jax
 import jax.numpy as jnp
 from jax import lax
+from jax.experimental import pallas as pl
+from jax.experimental.pallas import tpu as pltpu
 from jax.sharding import PartitionSpec as P
 
 HEAD = 56
@@ -191,53 +195,225 @@
         return jnp.concatenate([pick(x, mine, theirs), pick(x, theirs, mine)], axis=1)
 
 
-def weight_grad(links, left, right):
-    if not links.direct:
-        grad = tdot(left, right).astype(bf16)
-        grad = lax.psum_scatter(grad, "narrow", scatter_dimension=0, tiled=True)
-        return lax.psum_scatter(grad, "wide", scatter_dimension=1, tiled=True).astype(f32)
-    x, y, z, core = links.x, links.y, links.z, links.core
-    rows, columns = left.shape[1], right.shape[1]
-    half = rows // 2
-    unit = columns // 8
-    right_own = pick(core, right[:, : columns // 2], right[:, columns // 2 :])
-    right_away = pick(core, right[:, columns // 2 :], right[:, : columns // 2])
-    right_all = jnp.concatenate([right_own, links.over_core(right_away)], axis=0)
-    left_all = jnp.concatenate([left, links.over_core(left)], axis=0)
-    left_own = pick(x, left_all[:, :half], left_all[:, half:])
-    left_away = pick(x, left_all[:, half:], left_all[:, :half])
-    cut = [right_all[:, k * unit : (k + 1) * unit] for k in range(4)]
-    near = [pick(y, cut[0], cut[1]), pick(y, cut[2], cut[3])]
-    far = [pick(y, cut[1], cut[0]), pick(y, cut[3], cut[2])]
-
-    def both(one, two):
-        return jnp.stack([one.astype(bf16), two.astype(bf16)])
-
-    got_x = links.over_x(both(tdot(far[0], left_away), tdot(near[0], left_away)))
-    got_y = links.over_y(both(tdot(far[1], left_away), tdot(far[1], left_own)))
-    sum_far = tdot(far[0], left_own) + got_x[0].astype(f32)
-    even = tdot(near[0], left_own) + got_x[1].astype(f32)
-    sum_away = tdot(near[1], left_away) + got_y[0].astype(f32)
-    odd = tdot(near[1], left_own) + got_y[1].astype(f32)
-    even = even + links.over_y(sum_far.astype(bf16)).astype(f32)
-    odd = odd + links.over_x(sum_away.astype(bf16)).astype(f32)
-    low = z % 2 == 0
-    even_b, odd_b = even.astype(bf16), odd.astype(bf16)
-    same = jnp.where(low, odd_b, even_b)
-    straight = jnp.where(low, even_b, odd_b)
-    got_1 = links.send(same, lambda x, y, z, c: (x, y, z ^ 1, c) if z // 2 == c else None)
-    got_2 = links.send(straight, lambda x, y, z, c: (x, y, z ^ 2, c) if z // 2 != c else None)
-    got_3 = links.send(same, lambda x, y, z, c: (x, y, z ^ 3, c) if z // 2 != c else None)
-    total = jnp.where(low, even, odd)
-    total = total + got_1.astype(f32) + got_2.astype(f32) + got_3.astype(f32)
-    part = unit // 2
-    zero_part, one_part = total[:part], total[part:]
-    got = links.send(
-        pick(core, one_part, zero_part),
-        lambda x, y, z, c: (x, y, z, 1 - c) if z // 2 == c else None,
-    )
-    result = jnp.where(z // 2 == core, pick(core, zero_part, one_part), got)
-    return result.T
+MESH = pl.DeviceIdType.MESH
+
+
+def generic_grad(links, left, right):
+    grad = tdot(left, right).astype(bf16)
+    grad = lax.psum_scatter(grad, "narrow", scatter_dimension=0, tiled=True)
+    return lax.psum_scatter(grad, "wide", scatter_dimension=1, tiled=True).astype(f32)
+
+
+def reduce_kernel(count, *refs):
+    lefts = refs[:count]
+    rights = refs[count : 2 * count]
+    vec_ref = refs[2 * count]
+    outs = refs[2 * count + 1 : 3 * count + 1]
+    vec_out = refs[3 * count + 1]
+    rest = refs[3 * count + 2 :]
+    per = 12
+    bufs = [rest[k * per : (k + 1) * per] for k in range(count)]
+    vec_got, vec_sum, send_sem, recv_sem = rest[count * per :]
+    x = lax.axis_index("narrow")
+    spot = lax.axis_index("wide")
+    core = spot % 2
+    y = (spot // 2) % 2
+    z = spot // 4
+    over_x = {"narrow": 1 - x}
+    over_y = {"wide": spot + 2 - 4 * y}
+    over_core = {"wide": spot + 1 - 2 * core}
+    z_of = [z + 1 - 2 * (z % 2), z + 2 - 4 * (z // 2), 3 - z]
+    over_z = [{"wide": spot + 4 * (to - z)} for to in z_of]
+    partners = [over_x, over_y, over_core] + over_z
+
+    barrier = pltpu.get_barrier_semaphore()
+    for partner in partners:
+        pl.semaphore_signal(barrier, inc=1, device_id=partner, device_id_type=MESH)
+    pl.semaphore_wait(barrier, len(partners))
+
+    used = [0]
+    started = []
+
+    def send(source, target, partner):
+        k = used[0]
+        used[0] += 1
+        copy = pltpu.make_async_remote_copy(
+            src_ref=source,
+            dst_ref=target,
+            send_sem=send_sem.at[k],
+            recv_sem=recv_sem.at[k],
+            device_id=partner,
+            device_id_type=MESH,
+        )
+        copy.start()
+        started.append(copy)
+        return copy
+
+    from_core = []
+    for k in range(count):
+        left_pair, right_pair = bufs[k][0], bufs[k][1]
+        from_core.append(
+            (
+                send(lefts[k], left_pair, over_core),
+                send(rights[k].at[1 - core], right_pair, over_core),
+            )
+        )
+    steps = [over_core, over_x, over_y, over_z[0], over_z[1]]
+    vec_sum[0] = vec_ref[...]
+    vec_copy = [send(vec_sum.at[0], vec_got.at[0], steps[0])]
+
+    def vec_step(k):
+        vec_copy[-1].wait_recv()
+        vec_sum[k + 1] = vec_sum[k] + vec_got[k]
+        if k + 1 < len(steps):
+            vec_copy.append(send(vec_sum.at[k + 1], vec_got.at[k + 1], steps[k + 1]))
+
+    def unit(k, pair, side, away):
+        left_pair, right_pair = bufs[k][0], bufs[k][1]
+        rows = right_pair.shape[1] // 2
+        own = rights[k][core, side, pair * rows : (pair + 1) * rows, :]
+        other = right_pair[side, pair * rows : (pair + 1) * rows, :]
+        return jnp.dot(own, lefts[k][away], preferred_element_type=f32) + jnp.dot(
+            other, left_pair[away], preferred_element_type=f32
+        )
+
+    def phase1(k):
+        unused_l, unused_r, sx, sy, rx, ry = bufs[k][:6]
+
+        @pl.loop(0, 2)
+        def even(i):
+            sx[i] = unit(k, 0, (1 - y) + i * (2 * y - 1), 1).astype(bf16)
+
+        go_x = send(sx, rx, over_x)
+
+        @pl.loop(0, 2)
+        def odd(i):
+            sy[i] = unit(k, 1, 1 - y, 1 - i).astype(bf16)
+
+        go_y = send(sy, ry, over_y)
+        return go_x, go_y
+
+    def phase2(k, waits):
+        unused_l, unused_r, sx, sy, rx, ry, ty, tx, r2y, r2x = bufs[k][:10]
+        waits[0].wait_recv()
+        ty[...] = (unit(k, 0, 1 - y, 0) + rx[0].astype(f32)).astype(bf16)
+        go_y = send(ty, r2y, over_y)
+        waits[1].wait_recv()
+        tx[...] = (unit(k, 1, y, 1) + ry[0].astype(f32)).astype(bf16)
+        go_x = send(tx, r2x, over_x)
+        return go_y, go_x
+
+    def phase3(k, waits):
+        unused_l, unused_r, sx, sy, rx, ry, ty, tx, r2y, r2x, eo, rz = bufs[k]
+        block = eo.shape[1]
+        waits[0].wait_recv()
+        even = unit(k, 0, y, 0) + rx[1].astype(f32) + r2y[...].astype(f32)
+        eo[0] = even[:block].astype(bf16)
+        eo[1] = even[block:].astype(bf16)
+        waits[1].wait_recv()
+        odd = unit(k, 1, y, 0) + ry[1].astype(f32) + r2x[...].astype(f32)
+        eo[2] = odd[:block].astype(bf16)
+        eo[3] = odd[block:].astype(bf16)
+        return [send(eo.at[z_of[j]], rz.at[j], over_z[j]) for j in range(3)]
+
+    def phase4(k, waits):
+        eo, rz = bufs[k][10], bufs[k][11]
+        for copy in waits:
+            copy.wait_recv()
+        outs[k][...] = (
+            eo[z].astype(f32) + rz[0].astype(f32) + rz[1].astype(f32) + rz[2].astype(f32)
+        )
+
+    def from_pair(k):
+        for copy in from_core[k]:
+            copy.wait_recv()
+
+    first, second, third = {}, {}, {}
+    from_pair(0)
+    first[0] = phase1(0)
+    from_pair(1)
+    first[1] = phase1(1)
+    vec_step(0)
+    second[0] = phase2(0, first[0])
+    from_pair(3)
+    first[3] = phase1(3)
+    vec_step(1)
+    second[1] = phase2(1, first[1])
+    third[0] = phase3(0, second[0])
+    from_pair(2)
+    first[2] = phase1(2)
+    vec_step(2)
+    second[3] = phase2(3, first[3])
+    third[1] = phase3(1, second[1])
+    vec_step(3)
+    phase4(0, third[0])
+    second[2] = phase2(2, first[2])
+    third[3] = phase3(3, second[3])
+    phase4(1, third[1])
+    third[2] = phase3(2, second[2])
+    vec_step(4)
+    vec_out[...] = vec_sum[len(steps)]
+    phase4(3, third[3])
+    phase4(2, third[2])
+    for copy in started:
+        copy.wait_send()
+
+
+def reduce_all(links, pairs, vector):
+    lefts, rights, outs, scratch = [], [], [], []
+    flops = 0
+    for left, right in pairs:
+        rows, columns = left.shape[1], right.shape[1]
+        half, part = rows // 2, columns // 16
+        padded = -(-part // 8) * 8
+        lefts.append(
+            jnp.stack(
+                [
+                    pick(links.x, left[:, :half], left[:, half:]),
+                    pick(links.x, left[:, half:], left[:, :half]),
+                ]
+            )
+        )
+        tokens = right.shape[0]
+        blocks = right.T.reshape(4, 2, 2, part, tokens).transpose(2, 1, 0, 3, 4)
+        blocks = jnp.pad(blocks, ((0, 0), (0, 0), (0, 0), (0, padded - part), (0, 0)))
+        rights.append(blocks.reshape(2, 2, 4 * padded, tokens))
+        outs.append(jax.ShapeDtypeStruct((padded, half), f32))
+        wide = (2 * padded, half)
+        scratch += [
+            pltpu.VMEM((2, tokens, half), bf16),
+            pltpu.VMEM((2, 4 * padded, tokens), bf16),
+        ]
+        scratch += [pltpu.VMEM((2,) + wide, bf16)] * 4
+        scratch += [pltpu.VMEM(wide, bf16)] * 4
+        scratch += [pltpu.VMEM((4, padded, half), bf16), pltpu.VMEM((3, padded, half), bf16)]
+        flops += 2 * rows * columns * tokens
+    count = len(pairs)
+    copies = 9 * count + 5
+    scratch += [
+        pltpu.VMEM((5,) + vector.shape, f32),
+        pltpu.VMEM((6,) + vector.shape, f32),
+        pltpu.SemaphoreType.DMA((copies,)),
+        pltpu.SemaphoreType.DMA((copies,)),
+    ]
+    outs.append(jax.ShapeDtypeStruct(vector.shape, f32))
+    vmem = pl.BlockSpec(memory_space=pltpu.VMEM)
+    results = pl.pallas_call(
+        functools.partial(reduce_kernel, count),
+        out_shape=outs,
+        in_specs=[vmem] * (2 * count + 1),
+        out_specs=[vmem] * (count + 1),
+        scratch_shapes=scratch,
+        compiler_params=pltpu.CompilerParams(
+            collective_id=1, has_side_effects=True, vmem_limit_bytes=62 * 2**20
+        ),
+        cost_estimate=pl.CostEstimate(flops=flops, bytes_accessed=30 * 2**20, transcendentals=0),
+        name="reduce_grads",
+    )(*lefts, *rights, vector)
+    grads = []
+    for (left, right), out in zip(pairs, results):
+        grads.append(out[: right.shape[1] // 16].T)
+    return grads, results[-1]
 
 
 def gather_vectors(links, vectors):
@@ -256,16 +432,25 @@
     return full
 
 
-def vector_grads(links, sums):
+def all_grads(links, pairs, sums):
     lengths = [v.shape[0] for v in sums]
-    total = lax.psum(jnp.concatenate(sums), AXES)
+    width = min(lengths)
+    flat = jnp.concatenate(sums)
+    if links.direct:
+        rows = -(-sum(lengths) // (8 * width)) * 8
+        flat = jnp.pad(flat, (0, rows * width - sum(lengths))).reshape(rows, width)
+        grads, total = reduce_all(links, pairs, flat)
+        total = total.reshape(-1)
+    else:
+        grads = [generic_grad(links, left, right) for left, right in pairs]
+        total = lax.psum(flat, AXES)
     parts = []
     at = 0
     for length in lengths:
         own = length // links.count
         parts.append(lax.dynamic_slice_in_dim(total, at + links.x * own, own, 0))
         at += length
-    return parts
+    return grads, parts
 
 
 def local(
@@ -321,24 +506,20 @@
     second = normed(middle, gain2, shift2).astype(bf16)
     hidden = w_up.apply(second) + u_bias
     active = jax.nn.gelu(hidden, approximate=True).astype(bf16)
-    g_down = weight_grad(links, active, grad_out)
     result = middle + (w_down.apply(active) + d_bias)
     output = result.astype(bf16)[None]
 
     d_active = w_down.apply_t(grad_out)
     unused, gelu_pull = jax.vjp(lambda v: jax.nn.gelu(v, approximate=True), hidden)
     d_hidden = gelu_pull(d_active)[0].astype(bf16)
-    g_up = weight_grad(links, second, d_hidden)
     d_second = w_up.apply_t(d_hidden)
     unused, norm_pull = jax.vjp(normed, middle, gain2, shift2)
     d_middle, d_gain2, d_shift2 = norm_pull(d_second)
     d_middle = d_middle + grad_out.astype(f32)
     d_branch = d_middle.astype(bf16)
-    g_out = weight_grad(links, attended, d_branch)
     d_attended = w_out.apply_t(d_branch).astype(bf16)
     d_query, d_keys, d_values = attention_back(query, keys, values, logsum, d_attended, mask)
     d_mixed = jnp.concatenate([d_query, d_keys, d_values], axis=1)
-    g_qkv = weight_grad(links, first, d_mixed)
     d_first = w_qkv.apply_t(d_mixed)
     unused, first_pull = jax.vjp(normed, inputs, gain1, shift1)
     d_inputs, d_gain1, d_shift1 = first_pull(d_first)
@@ -347,8 +528,9 @@
     def column_sum(values):
         return jnp.sum(values.astype(f32), axis=0)
 
-    v_gain1, v_shift1, v_q, v_v, v_o, v_gain2, v_shift2, v_up, v_down = vector_grads(
+    grads, vectors = all_grads(
         links,
+        [(active, grad_out), (second, d_hidden), (attended, d_branch), (first, d_mixed)],
         [
             d_gain1,
             d_shift1,
@@ -361,6 +543,8 @@
             column_sum(grad_out),
         ],
     )
+    g_down, g_up, g_out, g_qkv = grads
+    v_gain1, v_shift1, v_q, v_v, v_o, v_gain2, v_shift2, v_up, v_down = vectors
     return (
         output,
         grad_tokens,

time: 580 us -> 521 us (0.90); the launches traced: 569 us -> 516 us
  Pallas kernels: 0 us -> 200 us
  waiting for transfers between devices: 260 us -> 107 us
  starting transfers between devices: 58.2 us -> 13.6 us
  blocking collectives: 40.1 us -> 0 us
  other arithmetic: 43 us -> 25.1 us
    pallas_call x0 -> x1, Pallas kernels: none -> 200 us  [reduce_all(): pl.pallas_call(functools.partial(reduce_kernel, count), out_shape=outs, i...]
    ppermute x57 -> x17, waiting for transfers between devices: 260 us -> 107 us  [send(): return lax.ppermute(value, AXES, self.table(move))]
    ppermute x57 -> x17, starting transfers between devices: 58.2 us -> 13.6 us  [send(): return lax.ppermute(value, AXES, self.table(move))]
    psum x1 -> x0, blocking collectives: 40.1 us -> none  [vector_grads(): total = lax.psum(jnp.concatenate(sums), AXES)]
    dot_general x32 -> x0, matrix products: 17.8 us -> none  [tdot(): lax.dot_general(left, right, (((0,), (0,)), ((), ())), preferred_element_...]
    select_n x15 -> x3, other arithmetic: 16.4 us -> 0.16 us  [pick(): return jnp.where(which == 0, zero, one)]
    transpose x0 -> x6, local copies, waits for them, and re-layouts: none -> 12.1 us  [the longest x3 8.44 us: reduce_all(): blocks = right.T.reshape(4, 2, 2, part, tokens).transpose(2, 1, 0, 3, 4)]
    dot_general x8, matrix products: 31.5 us -> 41.4 us  [dot(): return jnp.dot(left, right, preferred_element_type=f32)]
  transfers between devices with their start and end apart: 57 -> 17, of which waited for: 22 -> 6; matrix products, arithmetic and copies ran while one was open for 24% -> 14% of each run, Pallas kernels for 0% -> 0%
where the time goes in v2:
time: 521 us; the launch traced here: 516 us
  Pallas kernels  200 us (38%)
  waiting for transfers between devices  107 us (21%)
  matrix products  102 us (20%)
  local copies, waits for them, and re-layouts  57.4 us (11%)
  other arithmetic  25.1 us (5%)
  starting transfers between devices  13.6 us (3%)
  between operations  11 us (2%)
    pallas_call x1, Pallas kernels, reduce_all(): pl.pallas_call(functools.partial(reduce_kernel, count), out_shape=outs, i...  200 us
    ppermute x17, waiting for transfers between devices, send(): return lax.ppermute(value, AXES, self.table(move))  107 us
    dot_general x8, matrix products, dot(): return jnp.dot(left, right, preferred_element_type=f32)  41.4 us
    dot_general x8, matrix products, dot_t(): lax.dot_general(left, right, (((1,), (1,)), ((), ())), preferred_element_...  20 us
    ppermute x17, starting transfers between devices, send(): return lax.ppermute(value, AXES, self.table(move))  13.6 us
    unnamed x108, local copies, waits for them, and re-layouts  11.3 us
    dynamic_update_slice x16, local copies, waits for them, and re-layouts, gather_other(): whole = lax.dynamic_update_slice_in_dim(whole, value, spot, 0)  11.3 us
    dot_general x8, matrix products, scores_of(): jnp.einsum('qhe,khe->hqk', query, keys, preferred_element_type=f32)  11 us
  transfers between devices with their start and end apart: 17, of which 6 were waited for; matrix products, arithmetic and copies ran while one was open for 14% of the time, Pallas kernels for 0%

profile of v2, /device:TPU:0, one launch (start us, length us, event | category | flops | bytes accessed | tf_op | source)
XLA Modules:
  0.0 516.3 jit_solution(10907401041162833967)
XLA Ops:
  4.1 2.5 constant_dynamic-slice_fusion.1
  6.5 3.0 collective-permute-start.9
  10.4 2.2 constant_dynamic-slice_fusion.3
  12.6 2.0 collective-permute-start.1
  14.9 2.5 constant_dynamic-slice_fusion
  17.3 2.0 collective-permute-start.13
  21.4 5.7 %fusion.109 = f32[256,2240]{1,0:T(8,128)} fusion(bf16[2240,1120]{1,0:T(8,128)(2,1)} %param.40, bf16[1,256,1120]{1,2,0:T(8,128)(2,1)S(1)} %copy-done.16), kind=kOutput, calls=%fused_computation.151 | convolution fusion | flops 1284505600 | bytes 7884800 | tf_op jit(solution)/shard_map/dot_general | solution.py:27
  35.2 32.5 %collective-permute-done = bf16[6720]{0:T(1024)(128)(2,1)S(1)} collective-permute-done((bf16[6720]{0:T(1024)(128)(2,1)S(1)}, bf16[6720]{0:T(1024)(128)(2,1)S(1)}, u32[]{:S(2)}, u32[]{:S(2)}) %collective-permute-start) | collective-permute-done | bytes 13472 | tf_op jit(solution)/shard_map/ppermute | solution.py:126
  68.2 4.2 fusion.120
  73.9 2.1 collective-permute-start.6
  76.2 5.9 %collective-permute-done.6 = bf16[18,8,1120]{2,1,0:T(8,128)(2,1)S(1)} collective-permute-done((bf16[18,8,1120]{2,1,0:T(8,128)(2,1)S(1)}, bf16[18,8,1120]{2,1,0:T(8,128)(2,1)S(1)}, u32[]{:S(2)}, u32[]{:S(2)}) %collective-permute-start.6) | collective-permute-done | bytes 322592 | tf_op jit(solution)/shard_map/ppermute | solution.py:126
  82.2 1.6 collective-permute-start.2
  85.7 8.9 %collective-permute-done.13 = bf16[70,8,1120]{2,1,0:T(8,128)(2,1)} collective-permute-done((bf16[70,8,1120]{2,1,0:T(8,128)(2,1)}, bf16[70,8,1120]{2,1,0:T(8,128)(2,1)}, u32[]{:S(2)}, u32[]{:S(2)}) %collective-permute-start.13) | collective-permute-done | bytes 1254432 | tf_op jit(solution)/shard_map/ppermute | solution.py:126
  94.5 1.8 collective-permute-start.14
  100.4 7.0 %collective-permute-done.2 = bf16[18,8,3360]{2,1,0:T(8,128)(2,1)S(1)} collective-permute-done((bf16[18,8,3360]{2,1,0:T(8,128)(2,1)}, bf16[18,8,3360]{2,1,0:T(8,128)(2,1)S(1)}, u32[]{:S(2)}, u32[]{:S(2)}) %collective-permute-start.2) | collective-permute-done | bytes 967712 | tf_op jit(solution)/shard_map/ppermute | solution.py:126
  108.2 26.9 %collective-permute-done.14 = bf16[70,8,1120]{2,1,0:T(8,128)(2,1)} collective-permute-done((bf16[70,8,1120]{2,1,0:T(8,128)(2,1)}, bf16[70,8,1120]{2,1,0:T(8,128)(2,1)}, u32[]{:S(2)}, u32[]{:S(2)}) %collective-permute-start.14) | collective-permute-done | bytes 1254432 | tf_op jit(solution)/shard_map/ppermute | solution.py:126
  136.9 25.5 %collective-permute-done.10 = bf16[18,8,4480]{2,1,0:T(8,128)(2,1)} collective-permute-done((bf16[18,8,4480]{2,1,0:T(8,128)(2,1)}, bf16[18,8,4480]{2,1,0:T(8,128)(2,1)}, u32[]{:S(2)}, u32[]{:S(2)}) %collective-permute-start.10) | collective-permute-done | bytes 1290272 | tf_op jit(solution)/shard_map/ppermute | solution.py:126
  164.2 14.4 %convolution_add_fusion.1 = f32[256,3360]{0,1:T(8,128)S(1)} fusion(f32[256,3360]{0,1:T(8,128)S(1)} %fusion.120, bf16[70,8,3360]{2,1,0:T(8,128)(2,1)S(1)} %constant_dynamic-update-slice_fusion.12, pred[]{:T(512)S(6)} %eq.7, bf16[256,1120]{1,0:T(8,128)(2,1)S(1)} %fusion.101), kind=kOutput, calls=%fused_computation.70 | convolution fusion | flops 964382720 | bytes 11407361 | tf_op jit(solution)/shard_map/dot_general | solution.py:19
  180.1 11.7 %while.28 = (s32[]{:T(128)}, bf16[4,256,5,56]{1,3,2,0:T(8,128)(2,1)S(1)}, f32[4,5,256,1]{2,1,3,0:T(8,128)S(1)}, bf16[4,256,5,56]{1,3,2,0:T(8,128)(2,1)}, bf16[4,...) while((s32[]{:T(128)}, ...), condition=%wide.region_5.6_spmd.clone, body=%wide.region_2.5_spmd.clone.sunk | while | flops 76354304 | bytes 4695385 | solution.py:68
  194.8 2.5 fusion.137
  200.0 2.1 fusion.123
  202.1 1.7 constant_dynamic-update-slice_fusion
  204.1 1.8 broadcast_select_fusion.1
  208.2 6.8 %convert_reduce_fusion = (f32[4480]{0:T(1024)S(1)}, bf16[256,4480]{1,0:T(8,128)(2,1)S(1)}, bf16[256,4480]{1,0:T(8,128)(2,1)}) fusion(f32[256,2240]{1,0:T(8,128)S(1)} %get-tuple-element.260, f32[256,2240]{1,0:T(8,128)S(1)} %get-tuple-element.259, f32[4480]{0:T(1024)S(1)} %maximum_convert_fusion, f32[256,4480]{1,0:T(8,128)S(1)} %fusion.123, ...), kind=kOutput, calls=%fused_computation.86 | convolution fusion | flops 1315610240 | bytes 19604992 | tf_op jit(solution)/shard_map/dot_general | solution.py:19
  215.0 2.0 fusion.138
  217.1 2.0 broadcast_select_fusion.7
  227.2 32.0 %while.29 = (s32[]{:T(128)}, bf16[4,256,5,56]{1,3,2,0:T(8,128)(2,1)}, bf16[4,256,5,56]{1,3,2,0:T(8,128)(2,1)}, bf16[4,256,5,56]{1,3,2,0:T(8,128)(2,1)}, bf16[4,2...) while((s32[]{:T(128)}, ...), condition=%wide.region_12.13_spmd.clone, body=%wide.region_10.12_spmd.clone.sunk | while | flops 187069184 | bytes 11429233 | solution.py:90
  230.3 1.9 fusion.188
  233.1 1.9 fusion.189
  238.2 1.9 fusion.188
  241.0 1.9 fusion.189
  246.1 1.9 fusion.188
  248.9 1.9 fusion.189
  254.0 1.9 fusion.188
  256.9 1.9 fusion.189
  261.8 4.3 fusion.128
  266.1 2.5 fusion.127
  268.7 1.8 fusion.113
  270.5 5.4 %fusion.114 = f32[256,1120]{1,0:T(8,128)} fusion(bf16[2240,1120]{1,0:T(8,128)(2,1)} %param.40, pred[]{:T(512)S(6)} %eq.7, bf16[256,4480]{1,0:T(8,128)(2,1)S(1)} %copy-done.24), kind=kOutput, calls=%fused_computation.168 | convolution fusion | flops 1285079040 | bytes 8523777 | tf_op jit(solution)/shard_map/dot_general | solution.py:19
  275.9 2.7 broadcast_select_fusion.5
  281.0 3.0 convert_reduce_fusion.1
  286.3 1.7 copy.166
  290.2 4.2 copy.138
  294.4 3.2 copy.139
  299.9 1.6 pad_maximum_fusion.1.refs_0_
  302.4 199.9 %reduce_grads.1 = (f32[72,2240]{1,0:T(8,128)}, f32[280,560]{1,0:T(8,128)}, f32[72,560]{1,0:T(8,128)}, f32[216,560]{1,0:T(8,128)}, f32[16,1120]{1,0:T(8,128)}) custom-call(bf16[2,256,2240]{2,1,0:T(8,128)(2,1)} %pad_maximum_fusion.1.refs_0_, bf16[2,256,560]{2,1,0:T(8,128)(2,1)} %pad_maximum_fusion.5.refs_1_, bf16[2,256,560]{2,1,0:T(8,128)(2,1)} %pad_maximum_fusion.6.refs_2_, ...), custom_call_target="tpu_custom_call" | custom-call | flops 7707033600 | bytes 31457280 | tf_op jit(solution)/shard_map/reduce_grads/pallas_call | solution.py:401
  502.3 2.1 slice_bitcast_fusion
  507.5 5.3 %fusion.87 = bf16[1,256,1120]{2,1,0:T(8,128)(2,1)S(1)} fusion(f32[256,1120]{1,0:T(8,128)S(1)} %copy-done.5, f32[256,1120]{1,0:T(8,128)} %fusion.114, bf16[280,8,1120]{2,1,0:T(8,128)(2,1)} %copy-done.3, f32[1120]{0:T(1024)S(1)} %maximum_convert_fusion.8, pred[]{:T(512)S(6)} %eq.7, bf16[256,4480]{1,0:T(8,128)(2,1)} %get-tuple-element.261), kind=kOutput, calls=%fused_computation.99 | convolution fusion | flops 1286225920 | bytes 10424705 | tf_op jit(solution)/shard_map/dot_general | solution.py:19
  (265 shorter events, 82.2 us)
Async XLA Ops:
  0.6 8.9 %copy-start = (bf16[560,1120]{1,0:T(8,128)(2,1)S(1)}, bf16[560,1120]{1,0:T(8,128)(2,1)}, u32[]{:S(2)}) copy-start(bf16[560,1120]{1,0:T(8,128)(2,1)} %param.34) | copy-start | bytes 3763204
  6.5 91.7 %collective-permute-start.9 = (bf16[18,8,4480]{2,1,0:T(8,128)(2,1)}, bf16[18,8,4480]{2,1,0:T(8,128)(2,1)}, u32[]{:S(2)}, u32[]{:S(2)}) collective-permute-start(bf16[18,8,4480]{2,1,0:T(8,128)(2,1)} %constant_dynamic-slice_fusion.1), channel_id=1, source_target_pairs={{0,1},{1,0},{2,3},{3,2},{4,5},{5,4},{6,7},{7,6},{8,9},{9,8},{10,11... | collective-permute-start | bytes 3870728 | tf_op jit(solution)/shard_map/ppermute | solution.py:126
  9.5 5.1 copy-start.34
  9.5 5.1 copy-start.35
  9.5 5.1 copy-start.36
  9.5 5.1 copy-start.37
  9.5 5.1 copy-start.38
  9.5 5.1 copy-start.39
  9.6 5.1 copy-start.40
  9.6 5.1 copy-start.41
  9.6 5.1 copy-start.42
  10.3 63.5 %collective-permute-start.5 = (bf16[18,8,1120]{2,1,0:T(8,128)(2,1)}, bf16[18,8,1120]{2,1,0:T(8,128)(2,1)S(1)}, u32[]{:S(2)}, u32[]{:S(2)}) collective-permute-start(bf16[18,8,1120]{2,1,0:T(8,128)(2,1)} %constant_dynamic-slice_fusion.2), channel_id=1, source_target_pairs={{0,1},{1,0},{2,3},{3,2},{4,5},{5,4},{6,7},{7,6},{8,9},{9,8},{10,11... | collective-permute-start | bytes 967688 | tf_op jit(solution)/shard_map/ppermute | solution.py:126
  12.6 6.7 %copy-start.30 = (bf16[1,256,1120]{1,2,0:T(8,128)(2,1)S(1)}, bf16[1,256,1120]{1,2,0:T(8,128)(2,1)}, u32[]{:S(2)}) copy-start(bf16[1,256,1120]{1,2,0:T(8,128)(2,1)} %param.25) | copy-start | bytes 1720324
  12.6 69.6 %collective-permute-start.1 = (bf16[18,8,3360]{2,1,0:T(8,128)(2,1)}, bf16[18,8,3360]{2,1,0:T(8,128)(2,1)}, u32[]{:S(2)}, u32[]{:S(2)}) collective-permute-start(bf16[18,8,3360]{2,1,0:T(8,128)(2,1)} %constant_dynamic-slice_fusion.3), channel_id=1, source_target_pairs={{0,1},{1,0},{2,3},{3,2},{4,5},{5,4},{6,7},{7,6},{8,9},{9,8},{10,11... | collective-permute-start | bytes 2903048 | tf_op jit(solution)/shard_map/ppermute | solution.py:126
  14.8 52.9 %collective-permute-start = (bf16[6720]{0:T(1024)(128)(2,1)S(1)}, bf16[6720]{0:T(1024)(128)(2,1)S(1)}, u32[]{:S(2)}, u32[]{:S(2)}) collective-permute-start(bf16[6720]{0:T(1024)(128)(2,1)S(1)} %concatenate.90), channel_id=1, source_target_pairs={{0,1},{1,0},{2,3},{3,2},{4,5},{5,4},{6,7},{7,6},{8,9},{9,8},{10,11... | collective-permute-start | bytes 40328 | tf_op jit(solution)/shard_map/ppermute | solution.py:126
  17.3 4.1 copy-start.16
  17.3 77.2 %collective-permute-start.13 = (bf16[70,8,1120]{2,1,0:T(8,128)(2,1)}, bf16[70,8,1120]{2,1,0:T(8,128)(2,1)}, u32[]{:S(2)}, u32[]{:S(2)}) collective-permute-start(bf16[70,8,1120]{2,1,0:T(8,128)(2,1)} %constant_dynamic-slice_fusion), channel_id=1, source_target_pairs={{0,1},{1,0},{2,3},{3,2},{4,5},{5,4},{6,7},{7,6},{8,9},{9,8},{10,11... | collective-permute-start | bytes 3763208 | tf_op jit(solution)/shard_map/ppermute | solution.py:126
  73.9 8.2 %collective-permute-start.6 = (bf16[18,8,1120]{2,1,0:T(8,128)(2,1)S(1)}, bf16[18,8,1120]{2,1,0:T(8,128)(2,1)S(1)}, u32[]{:S(2)}, u32[]{:S(2)}) collective-permute-start(bf16[18,8,1120]{2,1,0:T(8,128)(2,1)S(1)} %collective-permute-done.5), channel_id=1, source_target_pairs={{0,4},{1,5},{2,6},{3,7},{4,0},{5,1},{6,2},{7,3},{8,12},{9,13},{10,... | collective-permute-start | bytes 967688 | tf_op jit(solution)/shard_map/ppermute | solution.py:126
  76.0 6.1 %collective-permute-start.7 = (bf16[18,8,1120]{2,1,0:T(8,128)(2,1)S(1)}, bf16[18,8,1120]{2,1,0:T(8,128)(2,1)S(1)}, u32[]{:S(2)}, u32[]{:S(2)}) collective-permute-start(bf16[18,8,1120]{2,1,0:T(8,128)(2,1)S(1)} %collective-permute-done.5), channel_id=1, source_target_pairs={{0,2},{1,3},{2,0},{3,1},{4,6},{5,7},{6,4},{7,5},{8,10},{9,11},{10,... | collective-permute-start | bytes 967688 | tf_op jit(solution)/shard_map/ppermute | solution.py:126
  82.1 3.5 collective-permute-start.8
  82.2 25.2 %collective-permute-start.2 = (bf16[18,8,3360]{2,1,0:T(8,128)(2,1)}, bf16[18,8,3360]{2,1,0:T(8,128)(2,1)S(1)}, u32[]{:S(2)}, u32[]{:S(2)}) collective-permute-start(bf16[18,8,3360]{2,1,0:T(8,128)(2,1)} %collective-permute-done.1), channel_id=1, source_target_pairs={{0,4},{1,5},{2,6},{3,7},{4,0},{5,1},{6,2},{7,3},{8,12},{9,13},{10,... | collective-permute-start | bytes 2903048 | tf_op jit(solution)/shard_map/ppermute | solution.py:126
  83.8 23.7 %collective-permute-start.3 = (bf16[18,8,3360]{2,1,0:T(8,128)(2,1)}, bf16[18,8,3360]{2,1,0:T(8,128)(2,1)S(1)}, u32[]{:S(2)}, u32[]{:S(2)}) collective-permute-start(bf16[18,8,3360]{2,1,0:T(8,128)(2,1)} %collective-permute-done.1), channel_id=1, source_target_pairs={{0,2},{1,3},{2,0},{3,1},{4,6},{5,7},{6,4},{7,5},{8,10},{9,11},{10,... | collective-permute-start | bytes 2903048 | tf_op jit(solution)/shard_map/ppermute | solution.py:126
  85.6 10.7 %copy-start.13 = (bf16[70,8,1120]{2,1,0:T(8,128)(2,1)}, bf16[70,8,1120]{2,1,0:T(8,128)(2,1)S(1)}, u32[]{:S(2)}) copy-start(bf16[70,8,1120]{2,1,0:T(8,128)(2,1)S(1)} %constant_dynamic-update-slice_fusion.8) | copy-start | bytes 3763204
  94.5 40.6 %collective-permute-start.14 = (bf16[70,8,1120]{2,1,0:T(8,128)(2,1)}, bf16[70,8,1120]{2,1,0:T(8,128)(2,1)}, u32[]{:S(2)}, u32[]{:S(2)}) collective-permute-start(bf16[70,8,1120]{2,1,0:T(8,128)(2,1)} %collective-permute-done.13), channel_id=1, source_target_pairs={{0,4},{1,5},{2,6},{3,7},{4,0},{5,1},{6,2},{7,3},{8,12},{9,13},{10,... | collective-permute-start | bytes 3763208 | tf_op jit(solution)/shard_map/ppermute | solution.py:126
  96.3 40.3 %collective-permute-start.15 = (bf16[70,8,1120]{2,1,0:T(8,128)(2,1)}, bf16[70,8,1120]{2,1,0:T(8,128)(2,1)S(1)}, u32[]{:S(2)}, u32[]{:S(2)}) collective-permute-start(bf16[70,8,1120]{2,1,0:T(8,128)(2,1)} %collective-permute-done.13), channel_id=1, source_target_pairs={{0,2},{1,3},{2,0},{3,1},{4,6},{5,7},{6,4},{7,5},{8,10},{9,11},{10,... | collective-permute-start | bytes 3763208 | tf_op jit(solution)/shard_map/ppermute | solution.py:126
  98.2 64.1 %collective-permute-start.10 = (bf16[18,8,4480]{2,1,0:T(8,128)(2,1)}, bf16[18,8,4480]{2,1,0:T(8,128)(2,1)}, u32[]{:S(2)}, u32[]{:S(2)}) collective-permute-start(bf16[18,8,4480]{2,1,0:T(8,128)(2,1)} %collective-permute-done.9), channel_id=1, source_target_pairs={{0,4},{1,5},{2,6},{3,7},{4,0},{5,1},{6,2},{7,3},{8,12},{9,13},{10,... | collective-permute-start | bytes 3870728 | tf_op jit(solution)/shard_map/ppermute | solution.py:126
  107.4 56.4 %collective-permute-start.11 = (bf16[18,8,4480]{2,1,0:T(8,128)(2,1)}, bf16[18,8,4480]{2,1,0:T(8,128)(2,1)S(1)}, u32[]{:S(2)}, u32[]{:S(2)}) collective-permute-start(bf16[18,8,4480]{2,1,0:T(8,128)(2,1)} %collective-permute-done.9), channel_id=1, source_target_pairs={{0,2},{1,3},{2,0},{3,1},{4,6},{5,7},{6,4},{7,5},{8,10},{9,11},{10,... | collective-permute-start | bytes 3870728 | tf_op jit(solution)/shard_map/ppermute | solution.py:126
  107.5 56.5 %collective-permute-start.4 = (bf16[18,8,3360]{2,1,0:T(8,128)(2,1)S(1)}, bf16[18,8,3360]{2,1,0:T(8,128)(2,1)S(1)}, u32[]{:S(2)}, u32[]{:S(2)}) collective-permute-start(bf16[18,8,3360]{2,1,0:T(8,128)(2,1)S(1)} %collective-permute-done.2), channel_id=1, source_target_pairs={{0,2},{1,3},{2,0},{3,1},{4,6},{5,7},{6,4},{7,5},{8,10},{9,11},{10,... | collective-permute-start | bytes 2903048 | tf_op jit(solution)/shard_map/ppermute | solution.py:126
  135.1 66.9 %collective-permute-start.16 = (bf16[70,8,1120]{2,1,0:T(8,128)(2,1)}, bf16[70,8,1120]{2,1,0:T(8,128)(2,1)}, u32[]{:S(2)}, u32[]{:S(2)}) collective-permute-start(bf16[70,8,1120]{2,1,0:T(8,128)(2,1)} %collective-permute-done.14), channel_id=1, source_target_pairs={{0,2},{1,3},{2,0},{3,1},{4,6},{5,7},{6,4},{7,5},{8,10},{9,11},{10,... | collective-permute-start | bytes 3763208 | tf_op jit(solution)/shard_map/ppermute | solution.py:126
  136.8 27.1 %copy-start.2 = (bf16[280,8,1120]{2,1,0:T(8,128)(2,1)}, bf16[280,8,1120]{2,1,0:T(8,128)(2,1)S(1)}, u32[]{:S(2)}) copy-start(bf16[280,8,1120]{2,1,0:T(8,128)(2,1)S(1)} %constant_dynamic-update-slice_fusion.1) | copy-start | bytes 15052804
  162.3 44.1 %collective-permute-start.12 = (bf16[18,8,4480]{2,1,0:T(8,128)(2,1)}, bf16[18,8,4480]{2,1,0:T(8,128)(2,1)}, u32[]{:S(2)}, u32[]{:S(2)}) collective-permute-start(bf16[18,8,4480]{2,1,0:T(8,128)(2,1)} %collective-permute-done.10), channel_id=1, source_target_pairs={{0,2},{1,3},{2,0},{3,1},{4,6},{5,7},{6,4},{7,5},{8,10},{9,11},{10,... | collective-permute-start | bytes 3870728 | tf_op jit(solution)/shard_map/ppermute | solution.py:126
  164.0 14.6 %copy-start.18 = (bf16[70,8,4480]{2,1,0:T(8,128)(2,1)}, bf16[70,8,4480]{2,1,0:T(8,128)(2,1)S(1)}, u32[]{:S(2)}) copy-start(bf16[70,8,4480]{2,1,0:T(8,128)(2,1)S(1)} %constant_dynamic-update-slice_fusion.5) | copy-start | bytes 15052804
  164.1 14.5 %copy-start.6 = (bf16[70,8,3360]{2,1,0:T(8,128)(2,1)}, bf16[70,8,3360]{2,1,0:T(8,128)(2,1)S(1)}, u32[]{:S(2)}) copy-start(bf16[70,8,3360]{2,1,0:T(8,128)(2,1)S(1)} %constant_dynamic-update-slice_fusion.12) | copy-start | bytes 11289604
  191.8 2.9 copy-start.9
  194.0 5.9 %slice-start.2 = ((s8[5017600]{0:T(1024)(128)(4,1)}), s8[4194304]{0:T(1024)(128)(4,1)S(1)}, s32[]{:S(2)}) async-start(s8[5017600]{0:T(1024)(128)(4,1)} %bitcast.289), calls=%async_computation.2 | async-start | bytes 8388608
  197.2 22.5 %copy-start.4 = (f32[256,1120]{1,0:T(8,128)}, f32[256,1120]{1,0:T(8,128)S(1)}, u32[]{:S(2)}) copy-start(f32[256,1120]{1,0:T(8,128)S(1)} %get-tuple-element.325) | copy-start | bytes 3440644
  199.0 3.1 slice-start
  200.0 3.8 copy-start.17
  202.1 4.3 slice-start.4
  223.7 3.5 copy-start.10
  261.8 4.4 copy-start.15
  261.8 4.4 copy-start.28
  270.5 5.4 %copy-start.7 = (bf16[70,8,3360]{2,1,0:T(8,128)(2,1)S(1)}, bf16[70,8,3360]{2,1,0:T(8,128)(2,1)}, u32[]{:S(2)}) copy-start(bf16[70,8,3360]{2,1,0:T(8,128)(2,1)} %copy-done.6) | copy-start | bytes 11289604
  280.9 3.9 copy-start.11
  502.3 3.0 copy-start.32
  502.3 3.7 copy-start.33
  502.3 3.8 copy-start.19
  507.5 8.6 %copy-start.1 = (bf16[560,1120]{1,0:T(8,128)(2,1)S(1)}, bf16[560,1120]{1,0:T(8,128)(2,1)}, u32[]{:S(2)}) copy-start(bf16[560,1120]{1,0:T(8,128)(2,1)} %param.34) | copy-start | bytes 3763204
  (18 other events, 37.0 us)
